TPU v7x, 256 devices: a whole 4x4x8 slice. The times are simulated.
256 devices in a mesh: feat: 32 (over y, z), dp: 8 (over x, core).
Axes of the slice: x: 4, y: 4, z: 8, core: 2. Of those that a mesh axis runs over, the one named last changes fastest.
Arguments:
- face_grid: bfloat16 [32768, 10240], P('dp', 'feat'), may hold values from -6 to 6
- first_nbrs: int32 [16384, 8], P('dp'), may hold values from 0 to 4095
- first_count: int32 [16384], P('dp'), may hold values from 1 to 8
- w_first: bfloat16 [10240, 256], P('feat'), may hold values from -0.0625 to 0.0625
- b_first: float32 [256], replicated, may hold values from -3 to 3
- send_rows: int32 [4096], P('dp'), may hold values from 0 to 2047
- second_nbrs: int32 [16384, 8], P(('dp', 'feat')), may hold values from 0 to 2559
- second_count: int32 [16384], P(('dp', 'feat')), may hold values from 1 to 8
- w_in: bfloat16 [256, 1024], replicated, may hold values from -0.375 to 0.375
- w_out: bfloat16 [1024, 256], replicated, may hold values from -0.1875 to 0.1875
- out_grad: bfloat16 [16384, 256], P(('dp', 'feat')), may hold values from -6 to 6
Outputs:
- embed: bfloat16 [16384, 256], P(('dp', 'feat'))
- grad_first: float32 [10240, 256], P('feat')
Inputs may be any that keep to these rules, and one draw needn't show every extreme that they name: `first_count`: slots at or past a target's count are ignored; counts lie in 1 to 8. `first_nbrs`: only slots below first_count are read. `second_count`: slots at or past a target's count are ignored. `second_nbrs`: indices below 2048 name the partition's own targets, the rest the faces received from the previous partition in order; only slots below second_count are read. `send_rows`: entries may repeat.
All inputs are finite; a program needn't handle non-finite values.
Results may differ from a plain program's by a relative error of at most 0.0061.
Values may be sent and summed in bfloat16 or wider, within the bound.
No kernel may reach another device: no remote copies, remote signals or barrier semaphores. Data moves between devices by JAX's collectives and lax.ppermute only.
A program may use at most 64 MiB of HBM per device.

v0:
```python
import jax
import jax.numpy as jnp
from jax import lax
from jax.sharding import PartitionSpec as P


def passed_along(shard, axis, by):
    devices = lax.axis_size(axis)
    return lax.ppermute(shard, axis, [(i, (i + by) % devices) for i in range(devices)])


def slope(value):
    sig = jax.nn.sigmoid(value)
    return sig * (1.0 + value * (1.0 - sig))


def mean_rows(table, nbrs, count):
    total = jnp.zeros((nbrs.shape[0], table.shape[1]), jnp.float32)
    for slot in range(nbrs.shape[1]):
        picked = table[nbrs[:, slot]].astype(jnp.float32)
        total = total + jnp.where((slot < count)[:, None], picked, 0.0)
    return total / count[:, None].astype(jnp.float32)


def spread(grad, nbrs, count, size):
    slots = jnp.arange(nbrs.shape[1], dtype=jnp.int32)
    factor = jnp.where(
        slots[None, :] < count[:, None], 1.0 / count[:, None].astype(jnp.float32), 0.0
    )
    terms = (grad[:, None, :] * factor[:, :, None]).reshape(-1, grad.shape[1])
    return jax.ops.segment_sum(terms, nbrs.reshape(-1), num_segments=size)


def body(
    face_grid,
    first_nbrs,
    first_count,
    w_first,
    b_first,
    send_rows,
    second_nbrs,
    second_count,
    w_in,
    w_out,
    out_grad,
):
    targets = first_nbrs.shape[0]
    agg_first = (
        face_grid[:targets].astype(jnp.float32) + mean_rows(face_grid, first_nbrs, first_count)
    ).astype(jnp.bfloat16)
    partial_value = jnp.dot(agg_first, w_first, preferred_element_type=jnp.float32)
    pre_own = lax.psum_scatter(partial_value, "feat", scatter_dimension=0, tiled=True) + b_first
    hidden_own = jax.nn.silu(pre_own).astype(jnp.bfloat16)
    table = lax.all_gather(hidden_own, "feat", axis=0, tiled=True)
    received = passed_along(table[send_rows], "dp", 1)
    extended = jnp.concatenate([table, received], axis=0)
    agg_second = (
        hidden_own.astype(jnp.float32) + mean_rows(extended, second_nbrs, second_count)
    ).astype(jnp.bfloat16)
    pre_mlp = jnp.dot(agg_second, w_in, preferred_element_type=jnp.float32)
    act_mlp = jax.nn.silu(pre_mlp).astype(jnp.bfloat16)
    embed = (
        hidden_own.astype(jnp.float32) + jnp.dot(act_mlp, w_out, preferred_element_type=jnp.float32)
    ).astype(jnp.bfloat16)
    grad_act = lax.dot_general(
        out_grad, w_out, (((1,), (1,)), ((), ())), preferred_element_type=jnp.float32
    )
    grad_pre_mlp = (grad_act * slope(pre_mlp)).astype(jnp.bfloat16)
    grad_agg = lax.dot_general(
        grad_pre_mlp, w_in, (((1,), (1,)), ((), ())), preferred_element_type=jnp.float32
    )
    grad_ext = spread(grad_agg, second_nbrs, second_count, extended.shape[0])
    full_rows = table.shape[0]
    returned = passed_along(grad_ext[full_rows:].astype(jnp.bfloat16), "dp", -1).astype(jnp.float32)
    table_grad = grad_ext[:full_rows].at[send_rows].add(returned)
    own_terms = out_grad.astype(jnp.float32) + grad_agg
    grad_own = (
        lax.psum_scatter(
            table_grad.astype(jnp.bfloat16), "feat", scatter_dimension=0, tiled=True
        ).astype(jnp.float32)
        + own_terms
    )
    grad_pre_own = (grad_own * slope(pre_own)).astype(jnp.bfloat16)
    grad_pre_first = lax.all_gather(grad_pre_own, "feat", axis=0, tiled=True)
    slice_grad = lax.dot_general(
        agg_first, grad_pre_first, (((0,), (0,)), ((), ())), preferred_element_type=jnp.float32
    )
    grad_first = lax.psum(slice_grad, "dp")
    return (embed, grad_first)


def solution(mesh):
    return jax.shard_map(
        body,
        mesh=mesh,
        in_specs=(
            P("dp", "feat"),
            P("dp", None),
            P("dp"),
            P("feat", None),
            P(),
            P("dp"),
            P(("dp", "feat"), None),
            P(("dp", "feat")),
            P(),
            P(),
            P(("dp", "feat"), None),
        ),
        out_specs=(P(("dp", "feat"), None), P("feat", None)),
        check_vma=False,
    )
```

profile of v0, /device:TPU:8, one launch (start us, length us, event | category | flops | bytes accessed | tf_op | source)
XLA Modules:
  0.0 828.4 jit_solution(5859287706951482798)
XLA Ops:
  8.7 4.6 copy.22
  13.4 11.2 %gather_fusion = bf16[2048,320]{1,0:T(8,128)(2,1)} fusion(bf16[4096,320]{1,0:T(8,128)(2,1)} %copy.22, s32[2048]{0:T(1024)S(1)} %broadcast_clamp_fusion.7), kind=kCustom, calls=%fused_computation | custom fusion | bytes 2629632 | tf_op jit(solution)/shard_map/gather | solution.py:20
  24.6 11.2 %gather_fusion.1 = bf16[2048,320]{1,0:T(8,128)(2,1)} fusion(bf16[4096,320]{1,0:T(8,128)(2,1)} %copy.22, s32[2048]{0:T(1024)S(1)} %broadcast_clamp_fusion.6), kind=kCustom, calls=%fused_computation.1 | custom fusion | bytes 2629632 | tf_op jit(solution)/shard_map/gather | solution.py:20
  35.8 11.2 %gather_fusion.2 = bf16[2048,320]{1,0:T(8,128)(2,1)} fusion(bf16[4096,320]{1,0:T(8,128)(2,1)} %copy.22, s32[2048]{0:T(1024)S(1)} %broadcast_clamp_fusion.5), kind=kCustom, calls=%fused_computation.2 | custom fusion | bytes 2629632 | tf_op jit(solution)/shard_map/gather | solution.py:20
  47.0 11.2 %gather_fusion.3 = bf16[2048,320]{1,0:T(8,128)(2,1)} fusion(bf16[4096,320]{1,0:T(8,128)(2,1)} %copy.22, s32[2048]{0:T(1024)S(1)} %broadcast_clamp_fusion.4), kind=kCustom, calls=%fused_computation.3 | custom fusion | bytes 2629632 | tf_op jit(solution)/shard_map/gather | solution.py:20
  58.1 11.2 %gather_fusion.4 = bf16[2048,320]{1,0:T(8,128)(2,1)} fusion(bf16[4096,320]{1,0:T(8,128)(2,1)} %copy.22, s32[2048]{0:T(1024)S(1)} %broadcast_clamp_fusion.3), kind=kCustom, calls=%fused_computation.4 | custom fusion | bytes 2629632 | tf_op jit(solution)/shard_map/gather | solution.py:20
  69.3 11.2 %gather_fusion.5 = bf16[2048,320]{1,0:T(8,128)(2,1)} fusion(bf16[4096,320]{1,0:T(8,128)(2,1)} %copy.22, s32[2048]{0:T(1024)S(1)} %broadcast_clamp_fusion.2), kind=kCustom, calls=%fused_computation.5 | custom fusion | bytes 2629632 | tf_op jit(solution)/shard_map/gather | solution.py:20
  80.5 11.2 %gather_fusion.6 = bf16[2048,320]{1,0:T(8,128)(2,1)} fusion(bf16[4096,320]{1,0:T(8,128)(2,1)} %copy.22, s32[2048]{0:T(1024)S(1)} %broadcast_clamp_fusion.1), kind=kCustom, calls=%fused_computation.6 | custom fusion | bytes 2629632 | tf_op jit(solution)/shard_map/gather | solution.py:20
  91.7 11.2 %gather_fusion.7 = bf16[2048,320]{1,0:T(8,128)(2,1)} fusion(bf16[4096,320]{1,0:T(8,128)(2,1)} %copy.22, s32[2048]{0:T(1024)S(1)} %broadcast_clamp_fusion), kind=kCustom, calls=%fused_computation.7 | custom fusion | bytes 2629632 | tf_op jit(solution)/shard_map/gather | solution.py:20
  102.8 8.9 %add_convert_fusion = bf16[2048,320]{1,0:T(8,128)(2,1)S(1)} fusion(bf16[2048,320]{1,0:T(8,128)(2,1)} %gather_fusion.7, bf16[2048,320]{1,0:T(8,128)(2,1)} %gather_fusion.6, bf16[2048,320]{1,0:T(8,128)(2,1)} %gather_fusion.5, bf16[2048,320]{1,0:T(8,128)(2,1)} %gather_fusion.4, bf16[2048,320]{1,0:T(8,128)(2,1)} %gather_fusion.3, ...), kind=kLoop, calls=%fused_computation.19 | loop fusion | flops 17694720 | bytes 13131776 | tf_op jit(solution)/shard_map/convert_element_type | solution.py:50
  111.8 2.0 fusion.40
  113.9 220.8 %reduce-scatter.3.cloned.1.call-done = f32[64,256]{1,0:T(8,128)} async-done(((f32[2048,256]{1,0:T(8,128)}), f32[64,256]{1,0:T(8,128)}) %reduce-scatter.3.cloned.1.call-update) | async-done | bytes 65552 | tf_op jit(solution)/shard_map/reduce_scatter | solution.py:52
  336.6 75.6 %all-gather.3.cloned.1.call-done = bf16[2048,256]{1,0:T(8,128)(2,1)} async-done(((bf16[64,256]{1,0:T(8,128)(2,1)}), bf16[2048,256]{1,0:T(8,128)(2,1)}) %all-gather.3.cloned.1.call-update) | async-done | bytes 1048592 | tf_op jit(solution)/shard_map/all_gather | solution.py:54
  412.2 3.6 gather_fusion.8
  417.3 5.8 collective-permute-done
  423.8 2.1 gather_fusion.10
  426.0 2.2 gather_fusion.11
  428.2 2.1 gather_fusion.12
  430.3 2.1 gather_fusion.13
  432.5 2.1 gather_fusion.14
  434.6 2.1 gather_fusion.15
  436.8 2.1 gather_fusion.9
  438.9 2.1 gather_fusion.16
  441.9 5.1 scatter_custom_fusion
  448.1 3.1 slice.112
  451.9 6.0 scatter_custom_fusion.1
  457.9 2.7 convert_element_type.125
  460.7 215.0 %reduce-scatter.5.cloned.1.call-done = bf16[64,256]{1,0:T(8,128)(2,1)} async-done(((bf16[2048,256]{1,0:T(8,128)(2,1)}), bf16[64,256]{1,0:T(8,128)(2,1)}) %reduce-scatter.5.cloned.1.call-update) | async-done | bytes 32784 | tf_op jit(solution)/shard_map/reduce_scatter | solution.py:78
  677.2 75.9 %all-gather.5.cloned.1.call-done = bf16[2048,256]{1,0:T(8,128)(2,1)} async-done(((bf16[64,256]{1,0:T(8,128)(2,1)}), bf16[2048,256]{1,0:T(8,128)(2,1)}) %all-gather.5.cloned.1.call-update) | async-done | bytes 1048592 | tf_op jit(solution)/shard_map/all_gather | solution.py:84
  753.1 2.5 fusion.41
  756.6 63.6 %all-reduce.2.cloned.1.call-done = f32[320,256]{1,0:T(8,128)} async-done(((f32[320,256]{1,0:T(8,128)}), f32[320,256]{1,0:T(8,128)}) %all-reduce.2.cloned.1.call-update) | async-done | bytes 327696 | tf_op jit(solution)/shard_map/psum | solution.py:88
  820.1 1.7 copy.35
  (70 shorter events, 10.7 us)
Async XLA Ops:
  7.2 433.9 %copy-start = (bf16[256,1024]{1,0:T(8,128)(2,1)S(1)}, bf16[256,1024]{1,0:T(8,128)(2,1)}, u32[]{:S(2)}) copy-start(bf16[256,1024]{1,0:T(8,128)(2,1)} %param.19) | copy-start | bytes 1572868
  7.2 327.5 %reduce-scatter.3.cloned.1.call-start = ((), (), s32[]{:S(2)}) async-start(), calls=%async_computation.2 | async-start | bytes 2162688 | tf_op jit(solution)/shard_map/reduce_scatter | solution.py:52
  8.7 4.6 copy-start.5
  102.8 8.9 %copy-start.3 = (bf16[320,256]{1,0:T(8,128)(2,1)S(1)}, bf16[320,256]{1,0:T(8,128)(2,1)}, u32[]{:S(2)}) copy-start(bf16[320,256]{1,0:T(8,128)(2,1)} %param.14) | copy-start | bytes 491524
  113.8 220.9 %copy-start.8 = (f32[256]{0:T(256)S(1)}, f32[256]{0:T(256)}, u32[]{:S(2)}) copy-start(f32[256]{0:T(256)} %param.15) | copy-start | bytes 3076
  113.8 222.6 %copy-start.10 = (s32[512]{0:T(512)S(1)}, s32[512]{0:T(512)}, u32[]{:S(2)}) copy-start(s32[512]{0:T(512)} %param.16) | copy-start | bytes 6148
  113.8 222.7 %copy-start.7 = (s32[64,8]{0,1:T(8,128)S(1)}, s32[64,8]{0,1:T(8,128)}, u32[]{:S(2)}) copy-start(s32[64,8]{0,1:T(8,128)} %param.17) | copy-start | bytes 6148
  113.8 222.7 %copy-start.9 = (s32[64]{0:T(128)S(1)}, s32[64]{0:T(128)}, u32[]{:S(2)}) copy-start(s32[64]{0:T(128)} %param.18) | copy-start | bytes 772
  113.8 298.4 %all-gather.3.cloned.1.call-start = ((), (), s32[]{:S(2)}) async-start(), calls=%async_computation.3 | async-start | bytes 1081344 | tf_op jit(solution)/shard_map/all_gather | solution.py:54
  336.2 339.6 %reduce-scatter.5.cloned.1.call-start = ((), (), s32[]{:S(2)}) async-start(), calls=%async_computation.4 | async-start | bytes 1081344 | tf_op jit(solution)/shard_map/reduce_scatter | solution.py:78
  412.2 3.9 copy-start.1
  415.9 7.2 collective-permute-start
  417.3 23.8 %copy-start.4 = (bf16[64,256]{1,0:T(8,128)(2,1)S(1)}, bf16[64,256]{1,0:T(8,128)(2,1)}, u32[]{:S(2)}) copy-start(bf16[64,256]{1,0:T(8,128)(2,1)} %multiply_convert_fusion.3) | copy-start | bytes 98308
  426.0 15.4 %copy-start.6 = (bf16[64,256]{1,0:T(8,128)(2,1)S(1)}, bf16[64,256]{1,0:T(8,128)(2,1)}, u32[]{:S(2)}) copy-start(bf16[64,256]{1,0:T(8,128)(2,1)} %param.21) | copy-start | bytes 98308
  426.0 15.4 %copy-start.11 = (bf16[1024,256]{1,0:T(8,128)(2,1)S(1)}, bf16[1024,256]{1,0:T(8,128)(2,1)}, u32[]{:S(2)}) copy-start(bf16[1024,256]{1,0:T(8,128)(2,1)} %param.20) | copy-start | bytes 1572868
  448.0 3.9 collective-permute-start.1
  457.9 217.8 %copy-start.2 = (f32[64,256]{1,0:T(8,128)S(1)}, f32[64,256]{1,0:T(8,128)}, u32[]{:S(2)}) copy-start(f32[64,256]{1,0:T(8,128)} %reduce-scatter.3.cloned.1.call-done) | copy-start | bytes 196612
  460.7 292.5 %all-gather.5.cloned.1.call-start = ((), (), s32[]{:S(2)}) async-start(), calls=%async_computation.5 | async-start | bytes 1081344 | tf_op jit(solution)/shard_map/all_gather | solution.py:84
  677.2 142.9 %all-reduce.2.cloned.1.call-start = ((), (), s32[]{:S(2)}) async-start(), calls=%async_computation.6 | async-start | bytes 655360 | tf_op jit(solution)/shard_map/psum | solution.py:88
Sparse Core Ops, SparseCore 0:
  113.9 220.6 reduce-scatter.2
  337.8 74.3 all-gather.2
  460.8 214.9 reduce-scatter.4
  678.8 74.3 all-gather.4
  755.9 64.2 all-reduce.1
where the time goes:
time: 830 us; the launch traced here: 828 us
  waiting for transfers between devices  658 us (79%)
  local copies, waits for them, and re-layouts  123 us (15%)
  other arithmetic  27.3 us (3%)
  between operations  14 us (2%)
    reduce_scatter x1, waiting for transfers between devices, body(): lax.psum_scatter(partial_value, 'feat', scatter_dimension=0, tiled=True)  221 us
    reduce_scatter x1, waiting for transfers between devices, body(): lax.psum_scatter(table_grad.astype(jnp.bfloat16), 'feat', scatter_dimensi...  215 us
    gather x16, local copies, waits for them, and re-layouts, mean_rows(): picked = table[nbrs[:, slot]].astype(jnp.float32)  107 us
    all_gather x1, waiting for transfers between devices, body(): grad_pre_first = lax.all_gather(grad_pre_own, 'feat', axis=0, tiled=True)  75.9 us
    all_gather x1, waiting for transfers between devices, body(): table = lax.all_gather(hidden_own, 'feat', axis=0, tiled=True)  75.6 us
    psum x1, waiting for transfers between devices, body(): grad_first = lax.psum(slice_grad, 'dp')  63.6 us
  transfers between devices with their start and end apart: 7, of which 7 were waited for; matrix products, arithmetic and copies ran while one was open for 1% of the time, Pallas kernels for 0%

commit v1 on v0

v1 whole, which is shorter than its diff:
```python
import functools

import jax
import jax.numpy as jnp
from jax import lax
from jax.experimental import pallas as pl
from jax.experimental.pallas import tpu as pltpu
from jax.sharding import Mesh, PartitionSpec as P


BF = jnp.bfloat16
F32 = jnp.float32
NY, NZ = 4, 8
BLOCK = 512
PIECE = BLOCK // NZ


def dot_nn(a, b):
    return lax.dot_general(a, b, (((1,), (0,)), ((), ())), preferred_element_type=F32)


def dot_nt(a, b):
    return lax.dot_general(a, b, (((1,), (1,)), ((), ())), preferred_element_type=F32)


def dot_tn(a, b):
    return lax.dot_general(a, b, (((0,), (0,)), ((), ())), preferred_element_type=F32)


def slope(value):
    half = 0.5 * jnp.tanh(0.5 * value)
    sig = 0.5 + half
    return sig * (1.0 + value * (0.5 - half))


def live_slots(nbrs, count):
    slot = lax.broadcasted_iota(jnp.int32, nbrs.shape, 0)
    idx = jnp.where(slot < count, nbrs, -1).astype(F32)
    mult = sum(jnp.where(idx == idx[k : k + 1], 1.0, 0.0) for k in range(nbrs.shape[0]))
    return idx, mult


def count_rows(idx, mult, base, rows):
    slots, width = idx.shape
    local = idx - base
    cols = [jnp.broadcast_to(local[k : k + 1, :], (16, width)).astype(BF) for k in range(slots)]
    vals = [jnp.broadcast_to(mult[k : k + 1, :], (16, width)).astype(BF) for k in range(slots)]
    row = lax.broadcasted_iota(jnp.int32, (16, width), 0).astype(F32)
    out = []
    for group in range(rows // 16):
        here = (row + float(16 * group)).astype(BF)
        acc = jnp.zeros((16, width), BF)
        for k in range(slots):
            acc = jnp.where(here == cols[k], vals[k], acc)
        out.append(acc)
    return jnp.concatenate(out, axis=0)


def whole(shape):
    return pl.BlockSpec(shape, lambda *_: (0,) * len(shape))


def grant(mib):
    return pltpu.CompilerParams(vmem_limit_bytes=mib << 20)


def cost(flops, moved):
    return pl.CostEstimate(flops=flops, bytes_accessed=moved, transcendentals=0)


def aggregate(block, face_ref, nbrs, count, w, ready, agg_ref, part_ref):
    width = agg_ref.shape[1]
    idx, mult = live_slots(nbrs, count)
    steps = face_ref.shape[1] // 512

    def half(h, total):
        for j in range(steps):
            at = 256 * (h * steps + j)
            counts = count_rows(idx, mult, at.astype(F32), 256)
            ready(h, 256 * j)
            faces = face_ref[:, pl.ds(pl.multiple_of(at, 256), 256)]
            total = total + dot_nn(faces, counts)
        return total

    total = lax.fori_loop(0, 2, half, jnp.zeros(agg_ref.shape, F32))
    start = pl.multiple_of(block * width, width)
    own = face_ref[:, pl.ds(start, width)].astype(F32)
    agg = (own + total * (1.0 / count.astype(F32))).astype(BF)
    agg_ref[...] = agg
    part_ref[...] = dot_tn(w, agg).astype(BF)


PIECES = 4


def chunk_body(block_ref, face_hbm, nbrs_hbm, count_hbm, w_hbm, *refs):
    outs, (face_ref, nbrs_ref, count_ref, w_ref, sems) = refs[:-5], refs[-5:]
    width = face_ref.shape[1] // PIECES
    small = [
        pltpu.make_async_copy(nbrs_hbm, nbrs_ref, sems.at[PIECES]),
        pltpu.make_async_copy(count_hbm, count_ref, sems.at[PIECES + 1]),
        pltpu.make_async_copy(w_hbm, w_ref, sems.at[PIECES + 2]),
    ]

    def big(i):
        cut = pl.ds(pl.multiple_of(i * width, width), width)
        return pltpu.make_async_copy(face_hbm.at[:, cut], face_ref.at[:, cut], sems.at[i])

    for copy in small + [big(i) for i in range(PIECES)]:
        copy.start()
    for copy in small:
        copy.wait()

    for i in range(len(outs) // 2):

        def ready(h, at):
            if i == 0 and at % width == 0:
                big(h * (PIECES // 2) + at // width).wait()

        block = block_ref[i]
        cut = pl.ds(pl.multiple_of(block * BLOCK, BLOCK), BLOCK)
        aggregate(
            block, face_ref, nbrs_ref[:, cut], count_ref[:, cut], w_ref[...], ready,
            outs[2 * i], outs[2 * i + 1],
        )


def agg_chunk(blocks, inputs):
    feats, hid = inputs[3].shape
    out = [((feats, BLOCK), BF), ((hid, BLOCK), BF)] * blocks.shape[0]
    spec = pltpu.PrefetchScalarGridSpec(
        num_scalar_prefetch=1,
        grid=(1,),
        in_specs=[pl.BlockSpec(memory_space=pltpu.HBM)] * len(inputs),
        out_specs=[whole(shape) for shape, _ in out],
        scratch_shapes=[pltpu.VMEM(v.shape, v.dtype) for v in inputs]
        + [pltpu.SemaphoreType.DMA((PIECES + 3,))],
    )
    work = 2 * BLOCK * feats * (inputs[0].shape[1] + hid) * blocks.shape[0]
    return pl.pallas_call(
        chunk_body,
        grid_spec=spec,
        out_shape=[jax.ShapeDtypeStruct(*v) for v in out],
        compiler_params=grant(60),
        cost_estimate=cost(work, 4 << 20),
        name="agg_chunk",
    )(blocks, *inputs)


def count_body(nbrs_ref, count_ref, out_ref, *, first):
    rows, width = out_ref.shape
    base = (first + pl.program_id(0) * rows).astype(F32)

    def step(c, carry):
        cut = pl.ds(pl.multiple_of(c * BLOCK, BLOCK), BLOCK)
        idx, mult = live_slots(nbrs_ref[:, cut], count_ref[:, cut])
        out_ref[:, cut] = count_rows(idx, mult, base, rows)
        return carry

    lax.fori_loop(0, width // BLOCK, step, 0)


def count_matrix(nbrs, count, first, rows, mib=12, step=256):
    slots, width = nbrs.shape
    return pl.pallas_call(
        functools.partial(count_body, first=first),
        grid=(rows // step,),
        in_specs=[whole((slots, width)), whole((1, width))],
        out_specs=pl.BlockSpec((step, width), lambda i: (i, 0)),
        out_shape=jax.ShapeDtypeStruct((rows, width), BF),
        compiler_params=grant(mib),
        cost_estimate=cost(slots * rows * width * 200, 2 * rows * width),
        name="count_matrix",
    )(nbrs, count)


def pack_body(nbrs_ref, count_ref, out_ref):
    nbrs = nbrs_ref[...]
    count = jnp.broadcast_to(count_ref[...], nbrs.shape)
    rows = jnp.concatenate([nbrs >> 8, nbrs & 255, count, jnp.zeros_like(nbrs)], axis=1)
    rows = jnp.concatenate([rows, jnp.zeros_like(rows)], axis=0).astype(F32).astype(BF)
    out_ref[...] = jnp.concatenate([rows, jnp.zeros_like(rows)], axis=1)


def pack(nbrs_t, count):
    shape = (16, BLOCK)
    return pl.pallas_call(
        pack_body,
        in_specs=[whole(v.shape) for v in (nbrs_t, count)],
        out_specs=whole(shape),
        grid=(1,),
        out_shape=jax.ShapeDtypeStruct(shape, BF),
        compiler_params=grant(12),
        name="pack",
    )(nbrs_t, count)


def unpack_body(y_ref, *refs):
    nbrs_ref, count_ref = refs[NY:]
    targets = nbrs_ref.shape[1]
    nbrs, count = [], []
    for d in range(NY):
        for z in range(NZ):
            rows = refs[d][z].astype(F32)[:8].astype(jnp.int32)
            nbrs.append(rows[:, :PIECE] * 256 + rows[:, PIECE : 2 * PIECE])
            count.append(rows[0:1, 2 * PIECE : 3 * PIECE])
    nbrs = jnp.concatenate(nbrs, axis=1)
    turned = (nbrs - y_ref[0] * BLOCK) & (targets - 1)
    nbrs_ref[...] = jnp.where(nbrs < targets, turned, nbrs)
    count_ref[...] = jnp.concatenate(count, axis=1)


def unpack(y, blocks):
    targets = NY * NZ * PIECE
    out = [((8, targets), jnp.int32), ((1, targets), jnp.int32)]
    spec = pltpu.PrefetchScalarGridSpec(
        num_scalar_prefetch=1,
        grid=(1,),
        in_specs=[whole(v.shape) for v in blocks],
        out_specs=[whole(shape) for shape, _ in out],
    )
    return pl.pallas_call(
        unpack_body,
        grid_spec=spec,
        out_shape=[jax.ShapeDtypeStruct(*v) for v in out],
        compiler_params=grant(12),
        name="unpack",
    )(y, *blocks)


def mlp_body(
    total_ref, received_ref, mat_ref, hidden_ref, count_ref, cot_ref, w_in_t_ref, w_in_ref, w_out_ref,
    agg_ref, grad_ref, shared_ref, back_ref, acc_ref,
):
    step = pl.program_id(0)
    inv = 1.0 / count_ref[...].astype(F32)
    total = total_ref[...] + dot_nn(received_ref[...], mat_ref[...])
    agg = (hidden_ref[...].astype(F32) + total * inv).astype(BF)

    @pl.when(step == 0)
    def _():
        agg_ref[...] = agg

    cot = cot_ref[...]
    grad = None
    inner = w_in_ref.shape[1] // 2
    for m in range(2):
        cut = slice(inner * m, inner * (m + 1))
        pre = dot_nn(w_in_t_ref[cut, :], agg)
        grad_act = dot_nt(w_out_ref[cut, :], cot)
        grad_pre = (grad_act * slope(pre)).astype(BF)
        term = dot_nn(w_in_ref[:, cut], grad_pre)
        grad = term if grad is None else grad + term
    grad_ref[...] = grad + cot.astype(F32).T
    shared = (grad * inv).astype(BF)
    shared_ref[...] = shared
    back = dot_nt(shared, mat_ref[...])

    @pl.when(step == 0)
    def _():
        acc_ref[...] = back

    @pl.when(step > 0)
    def _():
        acc_ref[...] += back

    @pl.when(step == NY - 1)
    def _():
        back_ref[...] = acc_ref[...].astype(BF)


def mlp(total, received, mat, hidden, count, cot, w_in_t, w_in, w_out):
    hid, targets = hidden.shape
    inner = w_in.shape[1]
    halo = received.shape[1]
    tile = pl.BlockSpec((hid, BLOCK), lambda i: (0, i))
    return pl.pallas_call(
        mlp_body,
        grid=(NY,),
        in_specs=[
            tile,
            whole((hid, halo)),
            pl.BlockSpec((halo, BLOCK), lambda i: (0, i)),
            tile,
            pl.BlockSpec((1, BLOCK), lambda i: (0, i)),
            pl.BlockSpec((BLOCK, hid), lambda i: (i, 0)),
            whole((inner, hid)),
            whole((hid, inner)),
            whole((inner, hid)),
        ],
        out_specs=[whole((hid, BLOCK)), tile, tile, whole((hid, halo))],
        out_shape=[
            jax.ShapeDtypeStruct((hid, BLOCK), BF),
            jax.ShapeDtypeStruct((hid, targets), F32),
            jax.ShapeDtypeStruct((hid, targets), BF),
            jax.ShapeDtypeStruct((hid, halo), BF),
        ],
        scratch_shapes=[pltpu.VMEM((hid, halo), F32)],
        cost_estimate=cost(4 * hid * targets * (inner + halo), 20 << 20),
        compiler_params=grant(20),
        name="mlp",
    )(total, received, mat, hidden, count, cot, w_in_t, w_in, w_out)


def last_body(core_ref, part_ref, returned_ref, pick_ref, *refs):
    pre_refs, agg_refs = refs[:NY], refs[NY : 2 * NY]
    keep_ref, give_ref, acc_ref = refs[2 * NY :]
    total = None
    for d in range(NY):
        cut = slice(BLOCK * d, BLOCK * (d + 1))
        grad = part_ref[:, cut] + dot_nt(returned_ref[...], pick_ref[cut, :])
        grad = (grad * slope(pre_refs[d][...].astype(F32))).astype(BF)
        term = dot_nt(agg_refs[d][...], grad)
        total = term if total is None else total + term
    acc_ref[...] = total
    half = keep_ref.shape[0]
    core = core_ref[0]
    keep_ref[...] = acc_ref[pl.ds(pl.multiple_of(core * half, half), half), :]
    give_ref[...] = acc_ref[pl.ds(pl.multiple_of((1 - core) * half, half), half), :]


def last(core, part, returned, pick, pre, agg):
    feats = agg[0].shape[0]
    hid = part.shape[0]
    out = jax.ShapeDtypeStruct((feats // 2, hid), F32)
    spec = pltpu.PrefetchScalarGridSpec(
        num_scalar_prefetch=1,
        grid=(1,),
        in_specs=[whole(v.shape) for v in (part, returned, pick, *pre, *agg)],
        out_specs=[whole(out.shape)] * 2,
        scratch_shapes=[pltpu.VMEM((feats, hid), F32)],
    )
    return pl.pallas_call(
        last_body, grid_spec=spec, out_shape=[out, out],
        cost_estimate=cost(4 << 30, 8 << 20), compiler_params=grant(16),
        name="last",
    )(core, part, returned, pick, *pre, *agg)


def shift(value, axis, by):
    devices = lax.axis_size(axis)
    return lax.ppermute(value, axis, [(i, (i + by) % devices) for i in range(devices)])


def swap(value, axis, bit):
    return lax.ppermute(value, axis, [(i, i ^ bit) for i in range(lax.axis_size(axis))])


def gather_z(piece):
    wide = jnp.broadcast_to(piece[None], (NZ,) + piece.shape)
    return lax.all_to_all(wide, "z", 0, 0).reshape(NZ * piece.shape[0], piece.shape[1])


def gather_y(own):
    return [own] + [shift(own, "y", NY - d) for d in range(1, NY)]


def body(
    face_grid,
    first_nbrs,
    first_count,
    w_first,
    b_first,
    send_rows,
    second_nbrs,
    second_count,
    w_in,
    w_out,
    out_grad,
):
    y, z = lax.axis_index("y"), lax.axis_index("z")
    core = lax.axis_index("core").astype(jnp.int32)
    targets = first_nbrs.shape[0]
    hid = w_first.shape[1]
    halo = send_rows.shape[0]

    inputs = [face_grid.T, first_nbrs.T, first_count[None, :], w_first]
    agg, got = {}, []
    for group in ((2,), (1, 3), (0,)):
        blocks = jnp.stack([((y + d) & (NY - 1)).astype(jnp.int32) for d in group])
        out = agg_chunk(blocks, inputs)
        for i, d in enumerate(group):
            agg[d], part = out[2 * i : 2 * i + 2]
            got.append(part if d == 0 else shift(part, "y", d))
    other = swap(out_grad, "z", 1)
    odd, second, third = (((z >> bit) & 1) == 1 for bit in range(3))
    pair = jnp.concatenate([out_grad, other], axis=0)
    pair = jnp.where(odd, jnp.concatenate([other, out_grad], axis=0), pair)
    others = [swap(pair, "z", bits) for bits in (2, 4, 6)]
    cot = jnp.stack([pair, *others]).reshape(2, 2, *pair.shape)
    cot = jnp.where(second, cot[:, ::-1], cot)
    cot = jnp.where(third, cot[::-1], cot).reshape(BLOCK, hid)

    lists = pack(second_nbrs.T, second_count[None, :])
    part_y = sum(g.astype(F32) for g in got).astype(BF).reshape(NZ, hid // NZ, BLOCK)
    part_y = jnp.concatenate(
        [part_y, jnp.broadcast_to(lists[None], (NZ,) + lists.shape)], axis=1
    )
    by_z = lax.all_to_all(part_y, "z", 0, 0)
    lists, by_z = by_z[:, hid // NZ :, : BLOCK // 2], by_z[:, : hid // NZ]
    bias = lax.dynamic_slice(b_first, (z * (hid // NZ),), (hid // NZ,))
    pre_own = (jnp.sum(by_z.astype(F32), axis=0) + bias[:, None]).astype(BF)
    pre = gather_z(pre_own)
    pre = gather_y(pre)

    lists = gather_y(lists)
    cot = gather_y(cot)
    nbrs2, count2 = unpack(y.astype(jnp.int32).reshape(1), lists)
    mat = count_matrix(nbrs2, count2, 0, targets)
    mat_halo = count_matrix(nbrs2, count2, targets, halo)
    cot = jnp.concatenate(cot, axis=0)
    rows = ((send_rows - y * BLOCK) & (targets - 1))[None, :]
    pick = count_matrix(rows, jnp.ones_like(rows), 0, targets)

    hidden = jax.nn.silu(jnp.concatenate(pre, axis=1).astype(F32)).astype(BF)
    received = shift(dot_nn(hidden, pick).astype(BF), ("x", "core"), 1)
    total = dot_nn(hidden, mat)
    agg2, grad_agg, shared, back = mlp(
        total, received, mat_halo, hidden, count2, cot, w_in.T, w_in, w_out
    )
    returned = shift(back, ("x", "core"), -1)
    grad_part = grad_agg + dot_nt(shared, mat)

    first = z * (BLOCK // NZ)
    own_agg = lax.dynamic_slice(agg2, (0, first), (hid, BLOCK // NZ))
    own_hidden = lax.dynamic_slice(hidden, (0, first), (hid, BLOCK // NZ))
    act = jax.nn.silu(dot_tn(own_agg, w_in)).astype(BF)
    embed = (own_hidden.T.astype(F32) + dot_nn(act, w_out)).astype(BF)

    keep, give = last(core.reshape(1), grad_part, returned, pick, pre, [agg[d] for d in range(NY)])
    pair = (keep + swap(give, "core", 1)).astype(BF)
    one, two, three = (swap(pair, "x", bit).astype(F32) for bit in (1, 2, 3))
    done = (pair.astype(F32) + one) + (two + three)
    done, embed = lax.optimization_barrier((done, embed))
    other = swap(done, "core", 1)
    grad_first = jnp.concatenate(
        [jnp.where(core == 0, done, other), jnp.where(core == 0, other, done)], axis=0
    )
    return embed, grad_first


def solution(mesh):
    fine = Mesh(mesh.devices.reshape(NY, NZ, 4, 2), ("y", "z", "x", "core"))
    feat, dp, every = ("y", "z"), ("x", "core"), ("x", "core", "y", "z")

    return jax.shard_map(
        body,
        mesh=fine,
        in_specs=(
            P(dp, feat),
            P(dp, None),
            P(dp),
            P(feat, None),
            P(),
            P(dp),
            P(every, None),
            P(every),
            P(),
            P(),
            P(every, None),
        ),
        out_specs=(P(every, None), P(feat, None)),
        check_vma=False,
    )
```

time: 830 us -> 127 us (0.15)
  waiting for transfers between devices: 658 us -> 24.1 us
  local copies, waits for them, and re-layouts: 123 us -> 3.29 us
  starting transfers between devices: 0.41 us -> 41.2 us
  Pallas kernels: 0 us -> 40.2 us
  other arithmetic: 27.3 us -> 7.57 us
  between operations: 14 us -> 1.08 us
    reduce_scatter x2 -> x0, waiting for transfers between devices: 436 us -> none  [the longest x1 221 us: body(): lax.psum_scatter(partial_value, 'feat', scatter_dimension=0, tiled=True)]
    all_gather x2 -> x0, waiting for transfers between devices: 151 us -> none  [the longest x1 75.9 us: body(): grad_pre_first = lax.all_gather(grad_pre_own, 'feat', axis=0, tiled=True)]
    gather x17 -> x0, local copies, waits for them, and re-layouts: 110 us -> none  [the longest x16 107 us: mean_rows(): picked = table[nbrs[:, slot]].astype(jnp.float32)]
    psum x1 -> x0, waiting for transfers between devices: 63.6 us -> none  [body(): grad_first = lax.psum(slice_grad, 'dp')]
    pallas_call x0 -> x10, Pallas kernels: none -> 40.2 us  [the longest x3 21 us: agg_chunk(): pl.pallas_call(chunk_body, grid_spec=spec, out_shape=[jax.ShapeDtypeStruc...]
    ppermute x2 -> x23, starting transfers between devices: 0.02 us -> 31.5 us  [the longest x14 16.3 us: shift(): lax.ppermute(value, axis, [(i, (i + by) % devices) for i in range(devices)])]
    convert_element_type x6 -> x4, other arithmetic: 15.2 us -> 2.71 us  [the longest x1 1.09 us: body(): sum((g.astype(F32) for g in got)).astype(BF).reshape(NZ, hid // NZ, BLOCK)]
    all_to_all x0 -> x2, waiting for transfers between devices: none -> 11.1 us  [the longest x1 8.57 us: body(): by_z = lax.all_to_all(part_y, 'z', 0, 0)]
  transfers between devices with their start and end apart: 7 -> 25, of which waited for: 7 -> 9; matrix products, arithmetic and copies ran while one was open for 1% -> 11% of each run, Pallas kernels for 0% -> 16%
where the time goes in v1:
time: 127 us; the launch traced here: 125 us
  starting transfers between devices  41.2 us (32%)
  Pallas kernels  40.2 us (32%)
  waiting for transfers between devices  24.1 us (19%)
  other arithmetic  7.57 us (6%)
  matrix products  7.19 us (6%)
  local copies, waits for them, and re-layouts  3.29 us (3%)
    pallas_call x3, Pallas kernels, agg_chunk(): pl.pallas_call(chunk_body, grid_spec=spec, out_shape=[jax.ShapeDtypeStruc...  21 us
    ppermute x14, starting transfers between devices, shift(): lax.ppermute(value, axis, [(i, (i + by) % devices) for i in range(devices)])  16.3 us
    ppermute x9, starting transfers between devices, swap(): lax.ppermute(value, axis, [(i, i ^ bit) for i in range(lax.axis_size(axis...  15.2 us
    pallas_call x1, Pallas kernels, mlp(): pl.pallas_call(mlp_body, grid=(NY,), in_specs=[tile, whole((hid, halo)),...  8.7 us
    all_to_all x1, waiting for transfers between devices, body(): by_z = lax.all_to_all(part_y, 'z', 0, 0)  8.57 us
    pallas_call x3, Pallas kernels, count_matrix(): pl.pallas_call(functools.partial(count_body, first=first), grid=(rows //...  8.21 us
    ppermute x14, waiting for transfers between devices, shift(): lax.ppermute(value, axis, [(i, (i + by) % devices) for i in range(devices)])  6.95 us
    all_to_all x1, starting transfers between devices, body(): by_z = lax.all_to_all(part_y, 'z', 0, 0)  6.29 us
  transfers between devices with their start and end apart: 25, of which 9 were waited for; matrix products, arithmetic and copies ran while one was open for 11% of the time, Pallas kernels for 16%

profile of v1, /device:TPU:8, one launch (start us, length us, event | category | flops | bytes accessed | tf_op | source)
XLA Modules:
  0.0 124.6 jit_solution(92772922866205335)
XLA Ops:
  1.3 9.8 %agg_chunk.4 = (bf16[320,512]{1,0:T(8,128)(2,1)}, bf16[256,512]{1,0:T(8,128)(2,1)}, bf16[320,512]{1,0:T(8,128)(2,1)}, bf16[256,512]{1,0:T(8,128)(2,1)}) custom-call(s32[2]{0:T(128)} %pad_add_fusion.block_ref, bf16[320,4096]{1,0:T(8,128)(2,1)} %bitcast.52, s32[8,2048]{1,0:T(8,128)} %bitcast.55, s32[1,2048]{1,0:T(1,128)} %bitcast.58, bf16[320,256]{1,0:T(8,128)(2,1)} %w_hbm.5), custom_call_target="tpu_custom_call" | custom-call | flops 2852126720 | bytes 4194304 | tf_op jit(solution)/shard_map/agg_chunk/pallas_call | solution.py:140
  11.1 1.7 %collective-permute-start.1 = (bf16[256,512]{1,0:T(8,128)(2,1)}, bf16[256,512]{1,0:T(8,128)(2,1)S(1)}, u32[]{:S(2)}, u32[]{:S(2)}) collective-permute-start(bf16[256,512]{1,0:T(8,128)(2,1)} %get-tuple-element.21), channel_id=1, source_target_pairs={{0,64},{64,128},{128,192},{192,0},{1,65},{65,129},{129,193},{193,1... | collective-permute-start | bytes 786440 | tf_op jit(solution)/shard_map/ppermute | solution.py:342
  13.5 5.6 %agg_chunk.3 = (bf16[320,512]{1,0:T(8,128)(2,1)}, bf16[256,512]{1,0:T(8,128)(2,1)}) custom-call(s32[1]{0:T(128)} %bitcast.1.block_ref, bf16[320,4096]{1,0:T(8,128)(2,1)} %bitcast.53, s32[8,2048]{1,0:T(8,128)} %bitcast.56, s32[1,2048]{1,0:T(1,128)} %bitcast.59, bf16[320,256]{1,0:T(8,128)(2,1)} %w_hbm.5), custom_call_target="tpu_custom_call" | custom-call | flops 1426063360 | bytes 4194304 | tf_op jit(solution)/shard_map/agg_chunk/pallas_call | solution.py:140
  19.0 2.1 %collective-permute-start = (bf16[256,512]{1,0:T(8,128)(2,1)}, bf16[256,512]{1,0:T(8,128)(2,1)S(1)}, u32[]{:S(2)}, u32[]{:S(2)}) collective-permute-start(bf16[256,512]{1,0:T(8,128)(2,1)} %get-tuple-element.20), channel_id=1, source_target_pairs={{0,128},{64,192},{128,0},{192,64},{1,129},{65,193},{129,1},{193,65... | collective-permute-start | bytes 786440 | tf_op jit(solution)/shard_map/ppermute | solution.py:342
  21.2 1.9 %collective-permute-start.10 = (bf16[64,256]{1,0:T(8,128)(2,1)S(1)}, bf16[64,256]{1,0:T(8,128)(2,1)S(1)}, u32[]{:S(2)}, u32[]{:S(2)}) collective-permute-start(bf16[64,256]{1,0:T(8,128)(2,1)S(1)} %copy-done.13), channel_id=1, source_target_pairs={{0,8},{8,0},{16,24},{24,16},{32,40},{40,32},{48,56},{56,48},{1,9},... | collective-permute-start | bytes 98312 | tf_op jit(solution)/shard_map/ppermute | solution.py:346
  23.1 5.6 %agg_chunk.5 = (bf16[320,512]{1,0:T(8,128)(2,1)}, bf16[256,512]{1,0:T(8,128)(2,1)}) custom-call(s32[1]{0:T(128)} %bitcast.7.block_ref, bf16[320,4096]{1,0:T(8,128)(2,1)} %bitcast.54, s32[8,2048]{1,0:T(8,128)} %bitcast.57, s32[1,2048]{1,0:T(1,128)} %bitcast.60, bf16[320,256]{1,0:T(8,128)(2,1)} %w_hbm.5), custom_call_target="tpu_custom_call" | custom-call | flops 1426063360 | bytes 4194304 | tf_op jit(solution)/shard_map/agg_chunk/pallas_call | solution.py:140
  29.9 3.4 %collective-permute-start.11 = (bf16[128,256]{1,0:T(8,128)(2,1)S(1)}, bf16[128,256]{1,0:T(8,128)(2,1)S(1)}, u32[]{:S(2)}, u32[]{:S(2)}) collective-permute-start(bf16[128,256]{1,0:T(8,128)(2,1)S(1)} %maximum_select_fusion.1), channel_id=1, source_target_pairs={{0,16},{8,24},{16,0},{24,8},{32,48},{40,56},{48,32},{56,40},{1,17}... | collective-permute-start | bytes 196616 | tf_op jit(solution)/shard_map/ppermute | solution.py:346
  33.3 4.5 %collective-permute-start.12 = (bf16[128,256]{1,0:T(8,128)(2,1)S(1)}, bf16[128,256]{1,0:T(8,128)(2,1)S(1)}, u32[]{:S(2)}, u32[]{:S(2)}) collective-permute-start(bf16[128,256]{1,0:T(8,128)(2,1)S(1)} %maximum_select_fusion.1), channel_id=1, source_target_pairs={{0,32},{8,40},{16,48},{24,56},{32,0},{40,8},{48,16},{56,24},{1,33}... | collective-permute-start | bytes 196616 | tf_op jit(solution)/shard_map/ppermute | solution.py:346
  39.7 6.3 %all-to-all-start = ((bf16[8,48,512]{2,1,0:T(8,128)(2,1)}), bf16[8,48,512]{2,1,0:T(8,128)(2,1)S(1)}, u32[]{:S(2)}, u32[]{:S(2)}) async-start(bf16[8,48,512]{2,1,0:T(8,128)(2,1)} %pad_maximum_fusion.1), calls=%async_computation | async-start | bytes 786432 | tf_op jit(solution)/shard_map/all_to_all | solution.py:399
  46.2 1.4 %collective-permute-start.14 = (bf16[512,256]{1,0:T(8,128)(2,1)S(1)}, bf16[512,256]{1,0:T(8,128)(2,1)S(1)}, u32[]{:S(2)}, u32[]{:S(2)}) collective-permute-start(bf16[512,256]{1,0:T(8,128)(2,1)S(1)} %bitcast.43), channel_id=1, source_target_pairs={{0,192},{64,0},{128,64},{192,128},{1,193},{65,1},{129,65},{193,129... | collective-permute-start | bytes 786440 | tf_op jit(solution)/shard_map/ppermute | solution.py:342
  48.6 1.6 %collective-permute-start.16 = (bf16[512,256]{1,0:T(8,128)(2,1)S(1)}, bf16[512,256]{1,0:T(8,128)(2,1)}, u32[]{:S(2)}, u32[]{:S(2)}) collective-permute-start(bf16[512,256]{1,0:T(8,128)(2,1)S(1)} %bitcast.45), channel_id=1, source_target_pairs={{0,64},{64,128},{128,192},{192,0},{1,65},{65,129},{129,193},{193,1... | collective-permute-start | bytes 786440 | tf_op jit(solution)/shard_map/ppermute | solution.py:342
  50.1 8.6 %all-to-all-done = bf16[8,48,512]{2,1,0:T(8,128)(2,1)S(1)} async-done(((bf16[8,48,512]{2,1,0:T(8,128)(2,1)}), bf16[8,48,512]{2,1,0:T(8,128)(2,1)S(1)}, u32[]{:S(2)}, u32[]{:S(2)}) %all-to-all-start) | async-done | bytes 393248 | tf_op jit(solution)/shard_map/all_to_all | solution.py:399
  59.6 3.4 %all-to-all-start.1 = ((bf16[8,32,512]{2,1,0:T(8,128)(2,1)}), bf16[8,32,512]{2,1,0:T(8,128)(2,1)S(1)}, u32[]{:S(2)}, u32[]{:S(2)}) async-start(bf16[8,32,512]{2,1,0:T(8,128)(2,1)} %broadcast_in_dim.28), calls=%async_computation.1 | async-start | bytes 524288 | tf_op jit(solution)/shard_map/all_to_all | solution.py:351
  63.4 1.4 %collective-permute-start.6 = (bf16[8,16,256]{2,1,0:T(8,128)(2,1)S(1)}, bf16[8,16,256]{2,1,0:T(8,128)(2,1)S(1)}, u32[]{:S(2)}, u32[]{:S(2)}) collective-permute-start(bf16[8,16,256]{2,1,0:T(8,128)(2,1)S(1)} %slice.9.refs_0_), channel_id=1, source_target_pairs={{0,192},{64,0},{128,64},{192,128},{1,193},{65,1},{129,65},{193,129... | collective-permute-start | bytes 196616 | tf_op jit(solution)/shard_map/ppermute | solution.py:342
  65.9 1.4 %collective-permute-start.8 = (bf16[8,16,256]{2,1,0:T(8,128)(2,1)S(1)}, bf16[8,16,256]{2,1,0:T(8,128)(2,1)S(1)}, u32[]{:S(2)}, u32[]{:S(2)}) collective-permute-start(bf16[8,16,256]{2,1,0:T(8,128)(2,1)S(1)} %slice.9.refs_0_), channel_id=1, source_target_pairs={{0,64},{64,128},{128,192},{192,0},{1,65},{65,129},{129,193},{193,1... | collective-permute-start | bytes 196616 | tf_op jit(solution)/shard_map/ppermute | solution.py:342
  67.4 2.1 %pad_maximum_fusion.cot_ref = bf16[2048,256]{1,0:T(8,128)(2,1)} fusion(bf16[512,256]{1,0:T(8,128)(2,1)} %collective-permute-done.16, bf16[512,256]{1,0:T(8,128)(2,1)} %collective-permute-done.15, bf16[512,256]{1,0:T(8,128)(2,1)S(1)} %collective-permute-done.14, bf16[512,256]{1,0:T(8,128)(2,1)S(1)} %bitcast.46), kind=kLoop, calls=%fused_computation.9 | loop fusion | flops 4194304 | bytes 2097152 | tf_op jit(solution)/shard_map/concatenate | solution.py:411
  70.8 2.6 %all-to-all-done.1 = bf16[8,32,512]{2,1,0:T(8,128)(2,1)S(1)} async-done(((bf16[8,32,512]{2,1,0:T(8,128)(2,1)}), bf16[8,32,512]{2,1,0:T(8,128)(2,1)S(1)}, u32[]{:S(2)}, u32[]{:S(2)}) %all-to-all-start.1) | async-done | bytes 262176 | tf_op jit(solution)/shard_map/all_to_all | solution.py:351
  73.4 1.4 %collective-permute-start.3 = (bf16[256,512]{1,0:T(8,128)(2,1)S(1)}, bf16[256,512]{1,0:T(8,128)(2,1)S(1)}, u32[]{:S(2)}, u32[]{:S(2)}) collective-permute-start(bf16[256,512]{1,0:T(8,128)(2,1)S(1)} %bitcast.32), channel_id=1, source_target_pairs={{0,192},{64,0},{128,64},{192,128},{1,193},{65,1},{129,65},{193,129... | collective-permute-start | bytes 786440 | tf_op jit(solution)/shard_map/ppermute | solution.py:342
  75.8 1.4 %collective-permute-start.5 = (bf16[256,512]{1,0:T(8,128)(2,1)S(1)}, bf16[256,512]{1,0:T(8,128)(2,1)S(1)}, u32[]{:S(2)}, u32[]{:S(2)}) collective-permute-start(bf16[256,512]{1,0:T(8,128)(2,1)S(1)} %bitcast.34), channel_id=1, source_target_pairs={{0,64},{64,128},{128,192},{192,0},{1,65},{65,129},{129,193},{193,1... | collective-permute-start | bytes 786440 | tf_op jit(solution)/shard_map/ppermute | solution.py:342
  77.2 6.2 %count_matrix.3 = bf16[2048,2048]{1,0:T(8,128)(2,1)S(1)} custom-call(s32[8,2048]{1,0:T(8,128)S(1)} %get-tuple-element.24.nbrs_ref, s32[1,2048]{1,0:T(1,128)S(1)} %get-tuple-element.25.count_ref), custom_call_target="tpu_custom_call" | custom-call | flops 6710886400 | bytes 8388608 | tf_op jit(solution)/shard_map/count_matrix/pallas_call | solution.py:165
  83.5 1.6 %count_matrix.5.mat_ref = bf16[512,2048]{1,0:T(8,128)(2,1)S(1)} custom-call(s32[8,2048]{1,0:T(8,128)S(1)} %get-tuple-element.24.nbrs_ref, s32[1,2048]{1,0:T(1,128)S(1)} %get-tuple-element.25.count_ref), custom_call_target="tpu_custom_call" | custom-call | flops 1677721600 | bytes 2097152 | tf_op jit(solution)/shard_map/count_matrix/pallas_call | solution.py:165
  86.5 2.3 %fusion.15.total_ref = f32[256,2048]{1,0:T(8,128)S(1)} fusion(bf16[256,2048]{1,0:T(8,128)(2,1)S(1)} %fusion.3.hidden_ref, bf16[2048,2048]{1,0:T(8,128)(2,1)S(1)} %count_matrix.3), kind=kOutput, calls=%fused_computation.32 | convolution fusion | flops 2147483648 | bytes 11534336 | tf_op jit(solution)/shard_map/dot_general | solution.py:19
  88.8 4.7 %collective-permute-done.9.received_ref = bf16[256,512]{1,0:T(8,128)(2,1)S(1)} collective-permute-done((bf16[256,512]{1,0:T(8,128)(2,1)S(1)}, bf16[256,512]{1,0:T(8,128)(2,1)S(1)}, u32[]{:S(2)}, u32[]{:S(2)}) %collective-permute-start.9) | collective-permute-done | bytes 262176 | tf_op jit(solution)/shard_map/ppermute | solution.py:342
  93.5 8.7 %mlp.1 = (bf16[256,512]{1,0:T(8,128)(2,1)S(1)}, f32[256,2048]{1,0:T(8,128)S(1)}, bf16[256,2048]{1,0:T(8,128)(2,1)S(1)}, bf16[256,512]{1,0:T(8,128)(2,1)S(1)}) custom-call(f32[256,2048]{1,0:T(8,128)S(1)} %fusion.15.total_ref, bf16[256,512]{1,0:T(8,128)(2,1)S(1)} %collective-permute-done.9.received_ref, bf16[512,2048]{1,0:T(8,128)(2,1)S(1)} %count_matrix.5.mat_ref, ...), custom_call_target="tpu_custom_call" | custom-call | flops 3221225472 | bytes 20971520 | tf_op jit(solution)/shard_map/mlp/pallas_call | solution.py:277
  102.2 2.4 %fusion.16 = f32[256,2048]{1,0:T(8,128)S(1)} fusion(bf16[256,2048]{1,0:T(8,128)(2,1)S(1)} %get-tuple-element.27, bf16[2048,2048]{1,0:T(8,128)(2,1)S(1)} %count_matrix.3), kind=kOutput, calls=%fused_computation.33 | convolution fusion | flops 2147483648 | bytes 11534336 | tf_op jit(solution)/shard_map/dot_general | solution.py:23
  106.1 2.1 %last.1 = (f32[160,256]{1,0:T(8,128)S(1)}, f32[160,256]{1,0:T(8,128)}) custom-call(s32[1]{0:T(128)} %bitcast.core_ref, f32[256,2048]{1,0:T(8,128)S(1)} %add.75.part_ref, bf16[256,512]{1,0:T(8,128)(2,1)S(1)} %collective-permute-done.17.returned_ref, bf16[2048,512]{1,0:T(8,128)(2,1)S(1)} %count_matrix.4.pick_ref, bf16[256,512]{1,0:T(8,128)(2,1)S(1)} %bitcast.36, ...), custom_call_target="tpu_custom_call" | custom-call | flops 4294967296 | bytes 8388608 | tf_op jit(solution)/shard_map/last/pallas_call | solution.py:333
  109.4 1.2 collective-permute-done.18
  111.6 1.6 %collective-permute-start.19 = (bf16[160,256]{1,0:T(8,128)(2,1)S(1)}, bf16[160,256]{1,0:T(8,128)(2,1)S(1)}, u32[]{:S(2)}, u32[]{:S(2)}) collective-permute-start(bf16[160,256]{1,0:T(8,128)(2,1)S(1)} %add_convert_fusion.1), channel_id=1, source_target_pairs={{0,2},{2,0},{4,6},{6,4},{1,3},{3,1},{5,7},{7,5},{8,10},{10,8},{12,... | collective-permute-start | bytes 245768 | tf_op jit(solution)/shard_map/ppermute | solution.py:346
  113.2 2.9 %collective-permute-start.20 = (bf16[160,256]{1,0:T(8,128)(2,1)S(1)}, bf16[160,256]{1,0:T(8,128)(2,1)S(1)}, u32[]{:S(2)}, u32[]{:S(2)}) collective-permute-start(bf16[160,256]{1,0:T(8,128)(2,1)S(1)} %add_convert_fusion.1), channel_id=1, source_target_pairs={{0,4},{2,6},{4,0},{6,2},{1,5},{3,7},{5,1},{7,3},{8,12},{10,14},{12... | collective-permute-start | bytes 245768 | tf_op jit(solution)/shard_map/ppermute | solution.py:346
  116.4 1.8 %fusion.4 = bf16[64,256]{0,1:T(8,128)(2,1)S(1)} fusion(bf16[1024,256]{1,0:T(8,128)(2,1)} %w_out_ref.1, bf16[256,1024]{1,0:T(8,128)(2,1)} %w_in_ref.1, bf16[256,512]{1,0:T(8,128)(2,1)} %copy-done.8, s32[]{:T(128)S(6)} %select_n.64, bf16[256,2048]{1,0:T(8,128)(2,1)S(1)} %fusion.3.hidden_ref, s32[]{:T(128)S(6)} %select_n.63), kind=kOutput, calls=%fused_computation.8 | convolution fusion | flops 67485696 | bytes 1179656 | tf_op jit(solution)/shard_map/dot_general | solution.py:19
  118.2 2.4 %collective-permute-done.20 = bf16[160,256]{1,0:T(8,128)(2,1)S(1)} collective-permute-done((bf16[160,256]{1,0:T(8,128)(2,1)S(1)}, bf16[160,256]{1,0:T(8,128)(2,1)S(1)}, u32[]{:S(2)}, u32[]{:S(2)}) %collective-permute-start.20) | collective-permute-done | bytes 81952 | tf_op jit(solution)/shard_map/ppermute | solution.py:346
  120.6 1.7 %collective-permute-done.21 = bf16[160,256]{1,0:T(8,128)(2,1)S(1)} collective-permute-done((bf16[160,256]{1,0:T(8,128)(2,1)S(1)}, bf16[160,256]{1,0:T(8,128)(2,1)S(1)}, u32[]{:S(2)}, u32[]{:S(2)}) %collective-permute-start.21) | collective-permute-done | bytes 81952 | tf_op jit(solution)/shard_map/ppermute | solution.py:346
  (89 shorter events, 17.8 us)
Async XLA Ops:
  11.1 26.7 %collective-permute-start.1 = (bf16[256,512]{1,0:T(8,128)(2,1)}, bf16[256,512]{1,0:T(8,128)(2,1)S(1)}, u32[]{:S(2)}, u32[]{:S(2)}) collective-permute-start(bf16[256,512]{1,0:T(8,128)(2,1)} %get-tuple-element.21), channel_id=1, source_target_pairs={{0,64},{64,128},{128,192},{192,0},{1,65},{65,129},{129,193},{193,1... | collective-permute-start | bytes 786440 | tf_op jit(solution)/shard_map/ppermute | solution.py:342
  12.8 25.0 %collective-permute-start.2 = (bf16[256,512]{1,0:T(8,128)(2,1)}, bf16[256,512]{1,0:T(8,128)(2,1)S(1)}, u32[]{:S(2)}, u32[]{:S(2)}) collective-permute-start(bf16[256,512]{1,0:T(8,128)(2,1)} %get-tuple-element.22), channel_id=1, source_target_pairs={{0,192},{64,0},{128,64},{192,128},{1,193},{65,1},{129,65},{193,129... | collective-permute-start | bytes 786440 | tf_op jit(solution)/shard_map/ppermute | solution.py:342
  13.5 7.7 %copy-start.13 = (bf16[64,256]{1,0:T(8,128)(2,1)S(1)}, bf16[64,256]{1,0:T(8,128)(2,1)}, u32[]{:S(2)}) copy-start(bf16[64,256]{1,0:T(8,128)(2,1)} %param.21) | copy-start | bytes 98308
  19.0 18.8 %collective-permute-start = (bf16[256,512]{1,0:T(8,128)(2,1)}, bf16[256,512]{1,0:T(8,128)(2,1)S(1)}, u32[]{:S(2)}, u32[]{:S(2)}) collective-permute-start(bf16[256,512]{1,0:T(8,128)(2,1)} %get-tuple-element.20), channel_id=1, source_target_pairs={{0,128},{64,192},{128,0},{192,64},{1,129},{65,193},{129,1},{193,65... | collective-permute-start | bytes 786440 | tf_op jit(solution)/shard_map/ppermute | solution.py:342
  21.2 8.7 %collective-permute-start.10 = (bf16[64,256]{1,0:T(8,128)(2,1)S(1)}, bf16[64,256]{1,0:T(8,128)(2,1)S(1)}, u32[]{:S(2)}, u32[]{:S(2)}) collective-permute-start(bf16[64,256]{1,0:T(8,128)(2,1)S(1)} %copy-done.13), channel_id=1, source_target_pairs={{0,8},{8,0},{16,24},{24,16},{32,40},{40,32},{48,56},{56,48},{1,9},... | collective-permute-start | bytes 98312 | tf_op jit(solution)/shard_map/ppermute | solution.py:346
  23.1 6.7 %copy-start.15 = (f32[256]{0:T(256)S(1)}, f32[256]{0:T(256)}, u32[]{:S(2)}) copy-start(f32[256]{0:T(256)} %param.15) | copy-start | bytes 3076
  29.9 16.1 %collective-permute-start.11 = (bf16[128,256]{1,0:T(8,128)(2,1)S(1)}, bf16[128,256]{1,0:T(8,128)(2,1)S(1)}, u32[]{:S(2)}, u32[]{:S(2)}) collective-permute-start(bf16[128,256]{1,0:T(8,128)(2,1)S(1)} %maximum_select_fusion.1), channel_id=1, source_target_pairs={{0,16},{8,24},{16,0},{24,8},{32,48},{40,56},{48,32},{56,40},{1,17}... | collective-permute-start | bytes 196616 | tf_op jit(solution)/shard_map/ppermute | solution.py:346
  33.3 12.7 %collective-permute-start.12 = (bf16[128,256]{1,0:T(8,128)(2,1)S(1)}, bf16[128,256]{1,0:T(8,128)(2,1)S(1)}, u32[]{:S(2)}, u32[]{:S(2)}) collective-permute-start(bf16[128,256]{1,0:T(8,128)(2,1)S(1)} %maximum_select_fusion.1), channel_id=1, source_target_pairs={{0,32},{8,40},{16,48},{24,56},{32,0},{40,8},{48,16},{56,24},{1,33}... | collective-permute-start | bytes 196616 | tf_op jit(solution)/shard_map/ppermute | solution.py:346
  37.8 8.2 %collective-permute-start.13 = (bf16[128,256]{1,0:T(8,128)(2,1)S(1)}, bf16[128,256]{1,0:T(8,128)(2,1)S(1)}, u32[]{:S(2)}, u32[]{:S(2)}) collective-permute-start(bf16[128,256]{1,0:T(8,128)(2,1)S(1)} %maximum_select_fusion.1), channel_id=1, source_target_pairs={{0,48},{8,56},{16,32},{24,40},{32,16},{40,24},{48,0},{56,8},{1,49}... | collective-permute-start | bytes 196616 | tf_op jit(solution)/shard_map/ppermute | solution.py:346
  38.9 24.1 %copy-start.14 = (s32[512]{0:T(512)S(1)}, s32[512]{0:T(512)}, u32[]{:S(2)}) copy-start(s32[512]{0:T(512)} %param.16) | copy-start | bytes 6148
  39.7 19.0 %all-to-all-start = ((bf16[8,48,512]{2,1,0:T(8,128)(2,1)}), bf16[8,48,512]{2,1,0:T(8,128)(2,1)S(1)}, u32[]{:S(2)}, u32[]{:S(2)}) async-start(bf16[8,48,512]{2,1,0:T(8,128)(2,1)} %pad_maximum_fusion.1), calls=%async_computation | async-start | bytes 786432 | tf_op jit(solution)/shard_map/all_to_all | solution.py:399
  46.2 19.8 %collective-permute-start.14 = (bf16[512,256]{1,0:T(8,128)(2,1)S(1)}, bf16[512,256]{1,0:T(8,128)(2,1)S(1)}, u32[]{:S(2)}, u32[]{:S(2)}) collective-permute-start(bf16[512,256]{1,0:T(8,128)(2,1)S(1)} %bitcast.43), channel_id=1, source_target_pairs={{0,192},{64,0},{128,64},{192,128},{1,193},{65,1},{129,65},{193,129... | collective-permute-start | bytes 786440 | tf_op jit(solution)/shard_map/ppermute | solution.py:342
  47.6 19.8 %collective-permute-start.15 = (bf16[512,256]{1,0:T(8,128)(2,1)S(1)}, bf16[512,256]{1,0:T(8,128)(2,1)}, u32[]{:S(2)}, u32[]{:S(2)}) collective-permute-start(bf16[512,256]{1,0:T(8,128)(2,1)S(1)} %bitcast.44), channel_id=1, source_target_pairs={{0,128},{64,192},{128,0},{192,64},{1,129},{65,193},{129,1},{193,65... | collective-permute-start | bytes 786440 | tf_op jit(solution)/shard_map/ppermute | solution.py:342
  48.6 18.8 %collective-permute-start.16 = (bf16[512,256]{1,0:T(8,128)(2,1)S(1)}, bf16[512,256]{1,0:T(8,128)(2,1)}, u32[]{:S(2)}, u32[]{:S(2)}) collective-permute-start(bf16[512,256]{1,0:T(8,128)(2,1)S(1)} %bitcast.45), channel_id=1, source_target_pairs={{0,64},{64,128},{128,192},{192,0},{1,65},{65,129},{129,193},{193,1... | collective-permute-start | bytes 786440 | tf_op jit(solution)/shard_map/ppermute | solution.py:342
  59.6 13.8 %all-to-all-start.1 = ((bf16[8,32,512]{2,1,0:T(8,128)(2,1)}), bf16[8,32,512]{2,1,0:T(8,128)(2,1)S(1)}, u32[]{:S(2)}, u32[]{:S(2)}) async-start(bf16[8,32,512]{2,1,0:T(8,128)(2,1)} %broadcast_in_dim.28), calls=%async_computation.1 | async-start | bytes 524288 | tf_op jit(solution)/shard_map/all_to_all | solution.py:351
  63.4 6.1 %collective-permute-start.6 = (bf16[8,16,256]{2,1,0:T(8,128)(2,1)S(1)}, bf16[8,16,256]{2,1,0:T(8,128)(2,1)S(1)}, u32[]{:S(2)}, u32[]{:S(2)}) collective-permute-start(bf16[8,16,256]{2,1,0:T(8,128)(2,1)S(1)} %slice.9.refs_0_), channel_id=1, source_target_pairs={{0,192},{64,0},{128,64},{192,128},{1,193},{65,1},{129,65},{193,129... | collective-permute-start | bytes 196616 | tf_op jit(solution)/shard_map/ppermute | solution.py:342
  64.9 5.8 %collective-permute-start.7 = (bf16[8,16,256]{2,1,0:T(8,128)(2,1)S(1)}, bf16[8,16,256]{2,1,0:T(8,128)(2,1)S(1)}, u32[]{:S(2)}, u32[]{:S(2)}) collective-permute-start(bf16[8,16,256]{2,1,0:T(8,128)(2,1)S(1)} %slice.9.refs_0_), channel_id=1, source_target_pairs={{0,128},{64,192},{128,0},{192,64},{1,129},{65,193},{129,1},{193,65... | collective-permute-start | bytes 196616 | tf_op jit(solution)/shard_map/ppermute | solution.py:342
  65.9 4.7 %collective-permute-start.8 = (bf16[8,16,256]{2,1,0:T(8,128)(2,1)S(1)}, bf16[8,16,256]{2,1,0:T(8,128)(2,1)S(1)}, u32[]{:S(2)}, u32[]{:S(2)}) collective-permute-start(bf16[8,16,256]{2,1,0:T(8,128)(2,1)S(1)} %slice.9.refs_0_), channel_id=1, source_target_pairs={{0,64},{64,128},{128,192},{192,0},{1,65},{65,129},{129,193},{193,1... | collective-permute-start | bytes 196616 | tf_op jit(solution)/shard_map/ppermute | solution.py:342
  73.4 11.7 %collective-permute-start.3 = (bf16[256,512]{1,0:T(8,128)(2,1)S(1)}, bf16[256,512]{1,0:T(8,128)(2,1)S(1)}, u32[]{:S(2)}, u32[]{:S(2)}) collective-permute-start(bf16[256,512]{1,0:T(8,128)(2,1)S(1)} %bitcast.32), channel_id=1, source_target_pairs={{0,192},{64,0},{128,64},{192,128},{1,193},{65,1},{129,65},{193,129... | collective-permute-start | bytes 786440 | tf_op jit(solution)/shard_map/ppermute | solution.py:342
  74.7 10.3 %collective-permute-start.4 = (bf16[256,512]{1,0:T(8,128)(2,1)S(1)}, bf16[256,512]{1,0:T(8,128)(2,1)S(1)}, u32[]{:S(2)}, u32[]{:S(2)}) collective-permute-start(bf16[256,512]{1,0:T(8,128)(2,1)S(1)} %bitcast.33), channel_id=1, source_target_pairs={{0,128},{64,192},{128,0},{192,64},{1,129},{65,193},{129,1},{193,65... | collective-permute-start | bytes 786440 | tf_op jit(solution)/shard_map/ppermute | solution.py:342
  75.8 9.3 %collective-permute-start.5 = (bf16[256,512]{1,0:T(8,128)(2,1)S(1)}, bf16[256,512]{1,0:T(8,128)(2,1)S(1)}, u32[]{:S(2)}, u32[]{:S(2)}) collective-permute-start(bf16[256,512]{1,0:T(8,128)(2,1)S(1)} %bitcast.34), channel_id=1, source_target_pairs={{0,64},{64,128},{128,192},{192,0},{1,65},{65,129},{129,193},{193,1... | collective-permute-start | bytes 786440 | tf_op jit(solution)/shard_map/ppermute | solution.py:342
  86.4 7.1 %copy-start = (bf16[2048,256]{1,0:T(8,128)(2,1)S(1)}, bf16[2048,256]{1,0:T(8,128)(2,1)}, u32[]{:S(2)}) copy-start(bf16[2048,256]{1,0:T(8,128)(2,1)} %pad_maximum_fusion.cot_ref) | copy-start | bytes 3145732
  86.4 7.1 %copy-start.2 = (bf16[256,1024]{1,0:T(8,128)(2,1)S(1)}, bf16[256,1024]{1,0:T(8,128)(2,1)}, u32[]{:S(2)}) copy-start(bf16[256,1024]{1,0:T(8,128)(2,1)} %w_in_ref.1) | copy-start | bytes 1572868
  86.4 7.0 %copy-start.3 = (bf16[256,1024]{0,1:T(8,128)(2,1)S(1)}, bf16[256,1024]{0,1:T(8,128)(2,1)}, u32[]{:S(2)}) copy-start(bf16[256,1024]{0,1:T(8,128)(2,1)} %copy.13) | copy-start | bytes 1572868
  86.4 7.0 %copy-start.7 = (bf16[1024,256]{1,0:T(8,128)(2,1)S(1)}, bf16[1024,256]{1,0:T(8,128)(2,1)}, u32[]{:S(2)}) copy-start(bf16[1024,256]{1,0:T(8,128)(2,1)} %w_out_ref.1) | copy-start | bytes 1572868
  86.5 7.0 %collective-permute-start.9 = (bf16[256,512]{1,0:T(8,128)(2,1)S(1)}, bf16[256,512]{1,0:T(8,128)(2,1)S(1)}, u32[]{:S(2)}, u32[]{:S(2)}) collective-permute-start(bf16[256,512]{1,0:T(8,128)(2,1)S(1)} %convolution_convert_fusion), channel_id=1, source_target_pairs={{0,1},{1,2},{2,3},{3,4},{4,5},{5,6},{6,7},{7,0},{8,9},{9,10},{10,1... | collective-permute-start | bytes 786440 | tf_op jit(solution)/shard_map/ppermute | solution.py:342
  102.2 3.9 %collective-permute-start.17 = (bf16[256,512]{1,0:T(8,128)(2,1)S(1)}, bf16[256,512]{1,0:T(8,128)(2,1)S(1)}, u32[]{:S(2)}, u32[]{:S(2)}) collective-permute-start(bf16[256,512]{1,0:T(8,128)(2,1)S(1)} %get-tuple-element.28), channel_id=1, source_target_pairs={{0,7},{1,0},{2,1},{3,2},{4,3},{5,4},{6,5},{7,6},{8,15},{9,8},{10,9... | collective-permute-start | bytes 786440 | tf_op jit(solution)/shard_map/ppermute | solution.py:342
  108.9 1.8 %collective-permute-start.18 = (f32[160,256]{1,0:T(8,128)}, f32[160,256]{1,0:T(8,128)S(1)}, u32[]{:S(2)}, u32[]{:S(2)}) collective-permute-start(f32[160,256]{1,0:T(8,128)} %get-tuple-element.34), channel_id=1, source_target_pairs={{0,1},{1,0},{2,3},{3,2},{4,5},{5,4},{6,7},{7,6},{8,9},{9,8},{10,11... | collective-permute-start | bytes 491528 | tf_op jit(solution)/shard_map/ppermute | solution.py:346
  111.6 6.6 %collective-permute-start.19 = (bf16[160,256]{1,0:T(8,128)(2,1)S(1)}, bf16[160,256]{1,0:T(8,128)(2,1)S(1)}, u32[]{:S(2)}, u32[]{:S(2)}) collective-permute-start(bf16[160,256]{1,0:T(8,128)(2,1)S(1)} %add_convert_fusion.1), channel_id=1, source_target_pairs={{0,2},{2,0},{4,6},{6,4},{1,3},{3,1},{5,7},{7,5},{8,10},{10,8},{12,... | collective-permute-start | bytes 245768 | tf_op jit(solution)/shard_map/ppermute | solution.py:346
  113.2 7.4 %collective-permute-start.20 = (bf16[160,256]{1,0:T(8,128)(2,1)S(1)}, bf16[160,256]{1,0:T(8,128)(2,1)S(1)}, u32[]{:S(2)}, u32[]{:S(2)}) collective-permute-start(bf16[160,256]{1,0:T(8,128)(2,1)S(1)} %add_convert_fusion.1), channel_id=1, source_target_pairs={{0,4},{2,6},{4,0},{6,2},{1,5},{3,7},{5,1},{7,3},{8,12},{10,14},{12... | collective-permute-start | bytes 245768 | tf_op jit(solution)/shard_map/ppermute | solution.py:346
  116.1 6.2 %collective-permute-start.21 = (bf16[160,256]{1,0:T(8,128)(2,1)S(1)}, bf16[160,256]{1,0:T(8,128)(2,1)S(1)}, u32[]{:S(2)}, u32[]{:S(2)}) collective-permute-start(bf16[160,256]{1,0:T(8,128)(2,1)S(1)} %add_convert_fusion.1), channel_id=1, source_target_pairs={{0,6},{2,4},{4,2},{6,0},{1,7},{3,5},{5,3},{7,1},{8,14},{10,12},{12... | collective-permute-start | bytes 245768 | tf_op jit(solution)/shard_map/ppermute | solution.py:346
  122.3 1.5 %collective-permute-start.22 = (f32[160,256]{1,0:T(8,128)S(1)}, f32[160,256]{1,0:T(8,128)S(1)}, u32[]{:S(2)}, u32[]{:S(2)}) collective-permute-start(f32[160,256]{1,0:T(8,128)S(1)} %add_add_fusion), channel_id=1, source_target_pairs={{0,1},{1,0},{2,3},{3,2},{4,5},{5,4},{6,7},{7,6},{8,9},{9,8},{10,11... | collective-permute-start | bytes 491528 | tf_op jit(solution)/shard_map/ppermute | solution.py:346
  (9 other events, 28.0 us)

commit v2 on v1

--- a/solution.py
+++ b/solution.py
@@ -68,21 +68,22 @@
     return pl.CostEstimate(flops=flops, bytes_accessed=moved, transcendentals=0)
 
 
-def aggregate(block, face_ref, nbrs, count, w, ready, agg_ref, part_ref):
+def aggregate(block, face_ref, nbrs, count, w, ready, agg_ref, part_ref, looped):
     width = agg_ref.shape[1]
     idx, mult = live_slots(nbrs, count)
-    steps = face_ref.shape[1] // 512
-
-    def half(h, total):
-        for j in range(steps):
-            at = 256 * (h * steps + j)
-            counts = count_rows(idx, mult, at.astype(F32), 256)
-            ready(h, 256 * j)
-            faces = face_ref[:, pl.ds(pl.multiple_of(at, 256), 256)]
+    total = jnp.zeros(agg_ref.shape, F32)
+    loops, size = (2, face_ref.shape[1] // 2) if looped else (1, face_ref.shape[1])
+
+    def some(h, total):
+        for at in range(0, size, 256):
+            base = h * size + at
+            counts = count_rows(idx, mult, (base + jnp.int32(0)).astype(F32), 256)
+            ready(base, at)
+            faces = face_ref[:, pl.ds(pl.multiple_of(base, 256), 256)]
             total = total + dot_nn(faces, counts)
         return total
 
-    total = lax.fori_loop(0, 2, half, jnp.zeros(agg_ref.shape, F32))
+    total = lax.fori_loop(0, loops, some, total) if looped else some(0, total)
     start = pl.multiple_of(block * width, width)
     own = face_ref[:, pl.ds(start, width)].astype(F32)
     agg = (own + total * (1.0 / count.astype(F32))).astype(BF)
@@ -93,7 +94,7 @@
 PIECES = 4
 
 
-def chunk_body(block_ref, face_hbm, nbrs_hbm, count_hbm, w_hbm, *refs):
+def chunk_body(y_ref, face_hbm, nbrs_hbm, count_hbm, w_hbm, *refs, group):
     outs, (face_ref, nbrs_ref, count_ref, w_ref, sems) = refs[:-5], refs[-5:]
     width = face_ref.shape[1] // PIECES
     small = [
@@ -106,28 +107,28 @@
         cut = pl.ds(pl.multiple_of(i * width, width), width)
         return pltpu.make_async_copy(face_hbm.at[:, cut], face_ref.at[:, cut], sems.at[i])
 
-    for copy in small + [big(i) for i in range(PIECES)]:
+    for copy in small + [big(p) for p in range(PIECES)]:
         copy.start()
     for copy in small:
         copy.wait()
 
-    for i in range(len(outs) // 2):
-
-        def ready(h, at):
+    for i, d in enumerate(group):
+
+        def ready(base, at):
             if i == 0 and at % width == 0:
-                big(h * (PIECES // 2) + at // width).wait()
-
-        block = block_ref[i]
+                big(base // width).wait()
+
+        block = (y_ref[0] + d) & (NY - 1)
         cut = pl.ds(pl.multiple_of(block * BLOCK, BLOCK), BLOCK)
         aggregate(
             block, face_ref, nbrs_ref[:, cut], count_ref[:, cut], w_ref[...], ready,
-            outs[2 * i], outs[2 * i + 1],
+            outs[2 * i], outs[2 * i + 1], len(group) == 1,
         )
 
 
-def agg_chunk(blocks, inputs):
+def agg_chunk(y, inputs, group):
     feats, hid = inputs[3].shape
-    out = [((feats, BLOCK), BF), ((hid, BLOCK), BF)] * blocks.shape[0]
+    out = [((feats, BLOCK), BF), ((hid, BLOCK), BF)] * len(group)
     spec = pltpu.PrefetchScalarGridSpec(
         num_scalar_prefetch=1,
         grid=(1,),
@@ -136,15 +137,15 @@
         scratch_shapes=[pltpu.VMEM(v.shape, v.dtype) for v in inputs]
         + [pltpu.SemaphoreType.DMA((PIECES + 3,))],
     )
-    work = 2 * BLOCK * feats * (inputs[0].shape[1] + hid) * blocks.shape[0]
-    return pl.pallas_call(
-        chunk_body,
+    work = 2 * BLOCK * feats * (inputs[0].shape[1] + hid) * len(group)
+    return pl.pallas_call(
+        functools.partial(chunk_body, group=group),
         grid_spec=spec,
         out_shape=[jax.ShapeDtypeStruct(*v) for v in out],
         compiler_params=grant(60),
         cost_estimate=cost(work, 4 << 20),
         name="agg_chunk",
-    )(blocks, *inputs)
+    )(y, *inputs)
 
 
 def count_body(nbrs_ref, count_ref, out_ref, *, first):
@@ -243,8 +244,8 @@
 
     cot = cot_ref[...]
     grad = None
-    inner = w_in_ref.shape[1] // 2
-    for m in range(2):
+    inner = w_in_ref.shape[1]
+    for m in range(1):
         cut = slice(inner * m, inner * (m + 1))
         pre = dot_nn(w_in_t_ref[cut, :], agg)
         grad_act = dot_nt(w_out_ref[cut, :], cot)
@@ -375,10 +376,10 @@
     halo = send_rows.shape[0]
 
     inputs = [face_grid.T, first_nbrs.T, first_count[None, :], w_first]
+    y_ref = y.astype(jnp.int32).reshape(1)
     agg, got = {}, []
     for group in ((2,), (1, 3), (0,)):
-        blocks = jnp.stack([((y + d) & (NY - 1)).astype(jnp.int32) for d in group])
-        out = agg_chunk(blocks, inputs)
+        out = agg_chunk(y_ref, inputs, group)
         for i, d in enumerate(group):
             agg[d], part = out[2 * i : 2 * i + 2]
             got.append(part if d == 0 else shift(part, "y", d))
@@ -405,7 +406,7 @@
 
     lists = gather_y(lists)
     cot = gather_y(cot)
-    nbrs2, count2 = unpack(y.astype(jnp.int32).reshape(1), lists)
+    nbrs2, count2 = unpack(y_ref, lists)
     mat = count_matrix(nbrs2, count2, 0, targets)
     mat_halo = count_matrix(nbrs2, count2, targets, halo)
     cot = jnp.concatenate(cot, axis=0)

time: 127 us -> 124 us (0.976)
  the two profiles are of different devices: /device:TPU:8 before, /device:TPU:1 now
where the time goes in v2:
time: 124 us
  starting transfers between devices  46.2 us (37%)
  Pallas kernels  37.9 us (31%)
  waiting for transfers between devices  21.1 us (17%)
  matrix products  7.18 us (6%)
  other arithmetic  6.95 us (6%)
  local copies, waits for them, and re-layouts  3.3 us (3%)
    ppermute x14, starting transfers between devices, shift(): lax.ppermute(value, axis, [(i, (i + by) % devices) for i in range(devices)])  23.4 us
    pallas_call x3, Pallas kernels, agg_chunk(): pl.pallas_call(functools.partial(chunk_body, group=group), grid_spec=spec...  19.3 us
    ppermute x9, starting transfers between devices, swap(): lax.ppermute(value, axis, [(i, i ^ bit) for i in range(lax.axis_size(axis...  13.7 us
    all_to_all x1, waiting for transfers between devices, body(): by_z = lax.all_to_all(part_y, 'z', 0, 0)  8.8 us
    pallas_call x3, Pallas kernels, count_matrix(): pl.pallas_call(functools.partial(count_body, first=first), grid=(rows //...  8.21 us
    pallas_call x1, Pallas kernels, mlp(): pl.pallas_call(mlp_body, grid=(NY,), in_specs=[tile, whole((hid, halo)),...  8.07 us
    ppermute x9, waiting for transfers between devices, swap(): lax.ppermute(value, axis, [(i, i ^ bit) for i in range(lax.axis_size(axis...  6.29 us
    all_to_all x1, starting transfers between devices, body(): by_z = lax.all_to_all(part_y, 'z', 0, 0)  5.74 us
  transfers between devices with their start and end apart: 25, of which 10 were waited for; matrix products, arithmetic and copies ran while one was open for 11% of the time, Pallas kernels for 16%

profile of v2, /device:TPU:1, one launch (start us, length us, event | category | flops | bytes accessed | tf_op | source)
XLA Modules:
  0.0 123.8 jit_solution(10784689478709239536)
XLA Ops:
  0.6 8.2 %agg_chunk.4 = (bf16[320,512]{1,0:T(8,128)(2,1)}, bf16[256,512]{1,0:T(8,128)(2,1)}, bf16[320,512]{1,0:T(8,128)(2,1)}, bf16[256,512]{1,0:T(8,128)(2,1)}) custom-call(s32[1]{0:T(128)} %bitcast.1.y_ref, bf16[320,4096]{1,0:T(8,128)(2,1)} %bitcast.48, s32[8,2048]{1,0:T(8,128)} %bitcast.51, s32[1,2048]{1,0:T(1,128)} %bitcast.54, bf16[320,256]{1,0:T(8,128)(2,1)} %w_hbm.5), custom_call_target="tpu_custom_call" | custom-call | flops 2852126720 | bytes 4194304 | tf_op jit(solution)/shard_map/agg_chunk/pallas_call | solution.py:141
  8.9 2.2 %collective-permute-start.1 = (bf16[256,512]{1,0:T(8,128)(2,1)}, bf16[256,512]{1,0:T(8,128)(2,1)S(1)}, u32[]{:S(2)}, u32[]{:S(2)}) collective-permute-start(bf16[256,512]{1,0:T(8,128)(2,1)} %get-tuple-element.21), channel_id=1, source_target_pairs={{0,64},{64,128},{128,192},{192,0},{1,65},{65,129},{129,193},{193,1... | collective-permute-start | bytes 786440 | tf_op jit(solution)/shard_map/ppermute | solution.py:343
  11.1 1.5 %collective-permute-start.2 = (bf16[256,512]{1,0:T(8,128)(2,1)}, bf16[256,512]{1,0:T(8,128)(2,1)S(1)}, u32[]{:S(2)}, u32[]{:S(2)}) collective-permute-start(bf16[256,512]{1,0:T(8,128)(2,1)} %get-tuple-element.22), channel_id=1, source_target_pairs={{0,192},{64,0},{128,64},{192,128},{1,193},{65,1},{129,65},{193,129... | collective-permute-start | bytes 786440 | tf_op jit(solution)/shard_map/ppermute | solution.py:343
  12.6 5.5 %agg_chunk.3 = (bf16[320,512]{1,0:T(8,128)(2,1)}, bf16[256,512]{1,0:T(8,128)(2,1)}) custom-call(s32[1]{0:T(128)} %bitcast.1.y_ref, bf16[320,4096]{1,0:T(8,128)(2,1)} %bitcast.49, s32[8,2048]{1,0:T(8,128)} %bitcast.52, s32[1,2048]{1,0:T(1,128)} %bitcast.55, bf16[320,256]{1,0:T(8,128)(2,1)} %w_hbm.5), custom_call_target="tpu_custom_call" | custom-call | flops 1426063360 | bytes 4194304 | tf_op jit(solution)/shard_map/agg_chunk/pallas_call | solution.py:141
  18.2 1.6 %collective-permute-start = (bf16[256,512]{1,0:T(8,128)(2,1)}, bf16[256,512]{1,0:T(8,128)(2,1)S(1)}, u32[]{:S(2)}, u32[]{:S(2)}) collective-permute-start(bf16[256,512]{1,0:T(8,128)(2,1)} %get-tuple-element.20), channel_id=1, source_target_pairs={{0,128},{64,192},{128,0},{192,64},{1,129},{65,193},{129,1},{193,65... | collective-permute-start | bytes 786440 | tf_op jit(solution)/shard_map/ppermute | solution.py:343
  19.9 1.6 %collective-permute-start.10 = (bf16[64,256]{1,0:T(8,128)(2,1)S(1)}, bf16[64,256]{1,0:T(8,128)(2,1)S(1)}, u32[]{:S(2)}, u32[]{:S(2)}) collective-permute-start(bf16[64,256]{1,0:T(8,128)(2,1)S(1)} %copy-done.13), channel_id=1, source_target_pairs={{0,8},{8,0},{16,24},{24,16},{32,40},{40,32},{48,56},{56,48},{1,9},... | collective-permute-start | bytes 98312 | tf_op jit(solution)/shard_map/ppermute | solution.py:347
  21.5 5.5 %agg_chunk.5 = (bf16[320,512]{1,0:T(8,128)(2,1)}, bf16[256,512]{1,0:T(8,128)(2,1)}) custom-call(s32[1]{0:T(128)} %bitcast.1.y_ref, bf16[320,4096]{1,0:T(8,128)(2,1)} %bitcast.50, s32[8,2048]{1,0:T(8,128)} %bitcast.53, s32[1,2048]{1,0:T(1,128)} %bitcast.56, bf16[320,256]{1,0:T(8,128)(2,1)} %w_hbm.5), custom_call_target="tpu_custom_call" | custom-call | flops 1426063360 | bytes 4194304 | tf_op jit(solution)/shard_map/agg_chunk/pallas_call | solution.py:141
  28.2 3.1 %collective-permute-start.11 = (bf16[128,256]{1,0:T(8,128)(2,1)S(1)}, bf16[128,256]{1,0:T(8,128)(2,1)S(1)}, u32[]{:S(2)}, u32[]{:S(2)}) collective-permute-start(bf16[128,256]{1,0:T(8,128)(2,1)S(1)} %maximum_select_fusion.1), channel_id=1, source_target_pairs={{0,16},{8,24},{16,0},{24,8},{32,48},{40,56},{48,32},{56,40},{1,17}... | collective-permute-start | bytes 196616 | tf_op jit(solution)/shard_map/ppermute | solution.py:347
  31.3 4.2 %collective-permute-start.12 = (bf16[128,256]{1,0:T(8,128)(2,1)S(1)}, bf16[128,256]{1,0:T(8,128)(2,1)S(1)}, u32[]{:S(2)}, u32[]{:S(2)}) collective-permute-start(bf16[128,256]{1,0:T(8,128)(2,1)S(1)} %maximum_select_fusion.1), channel_id=1, source_target_pairs={{0,32},{8,40},{16,48},{24,56},{32,0},{40,8},{48,16},{56,24},{1,33}... | collective-permute-start | bytes 196616 | tf_op jit(solution)/shard_map/ppermute | solution.py:347
  37.4 5.7 %all-to-all-start = ((bf16[8,48,512]{2,1,0:T(8,128)(2,1)}), bf16[8,48,512]{2,1,0:T(8,128)(2,1)S(1)}, u32[]{:S(2)}, u32[]{:S(2)}) async-start(bf16[8,48,512]{2,1,0:T(8,128)(2,1)} %pad_maximum_fusion.1), calls=%async_computation | async-start | bytes 786432 | tf_op jit(solution)/shard_map/all_to_all | solution.py:400
  44.3 1.4 %collective-permute-start.15 = (bf16[512,256]{1,0:T(8,128)(2,1)S(1)}, bf16[512,256]{1,0:T(8,128)(2,1)}, u32[]{:S(2)}, u32[]{:S(2)}) collective-permute-start(bf16[512,256]{1,0:T(8,128)(2,1)S(1)} %bitcast.40), channel_id=1, source_target_pairs={{0,128},{64,192},{128,0},{192,64},{1,129},{65,193},{129,1},{193,65... | collective-permute-start | bytes 786440 | tf_op jit(solution)/shard_map/ppermute | solution.py:343
  45.8 8.8 %all-to-all-done = bf16[8,48,512]{2,1,0:T(8,128)(2,1)S(1)} async-done(((bf16[8,48,512]{2,1,0:T(8,128)(2,1)}), bf16[8,48,512]{2,1,0:T(8,128)(2,1)S(1)}, u32[]{:S(2)}, u32[]{:S(2)}) %all-to-all-start) | async-done | bytes 393248 | tf_op jit(solution)/shard_map/all_to_all | solution.py:400
  55.4 3.4 %all-to-all-start.1 = ((bf16[8,32,512]{2,1,0:T(8,128)(2,1)}), bf16[8,32,512]{2,1,0:T(8,128)(2,1)S(1)}, u32[]{:S(2)}, u32[]{:S(2)}) async-start(bf16[8,32,512]{2,1,0:T(8,128)(2,1)} %broadcast_in_dim.28), calls=%async_computation.1 | async-start | bytes 524288 | tf_op jit(solution)/shard_map/all_to_all | solution.py:352
  60.2 1.4 %collective-permute-start.7 = (bf16[8,16,256]{2,1,0:T(8,128)(2,1)S(1)}, bf16[8,16,256]{2,1,0:T(8,128)(2,1)S(1)}, u32[]{:S(2)}, u32[]{:S(2)}) collective-permute-start(bf16[8,16,256]{2,1,0:T(8,128)(2,1)S(1)} %slice.9.refs_0_), channel_id=1, source_target_pairs={{0,128},{64,192},{128,0},{192,64},{1,129},{65,193},{129,1},{193,65... | collective-permute-start | bytes 196616 | tf_op jit(solution)/shard_map/ppermute | solution.py:343
  61.9 2.1 %pad_maximum_fusion.cot_ref = bf16[2048,256]{1,0:T(8,128)(2,1)} fusion(bf16[512,256]{1,0:T(8,128)(2,1)} %collective-permute-done.16, bf16[512,256]{1,0:T(8,128)(2,1)} %collective-permute-done.15, bf16[512,256]{1,0:T(8,128)(2,1)S(1)} %collective-permute-done.14, bf16[512,256]{1,0:T(8,128)(2,1)S(1)} %bitcast.42), kind=kLoop, calls=%fused_computation.9 | loop fusion | flops 4194304 | bytes 2097152 | tf_op jit(solution)/shard_map/concatenate | solution.py:412
  66.1 2.0 %all-to-all-done.1 = bf16[8,32,512]{2,1,0:T(8,128)(2,1)S(1)} async-done(((bf16[8,32,512]{2,1,0:T(8,128)(2,1)}), bf16[8,32,512]{2,1,0:T(8,128)(2,1)S(1)}, u32[]{:S(2)}, u32[]{:S(2)}) %all-to-all-start.1) | async-done | bytes 262176 | tf_op jit(solution)/shard_map/all_to_all | solution.py:352
  68.9 1.4 %collective-permute-start.4 = (bf16[256,512]{1,0:T(8,128)(2,1)S(1)}, bf16[256,512]{1,0:T(8,128)(2,1)S(1)}, u32[]{:S(2)}, u32[]{:S(2)}) collective-permute-start(bf16[256,512]{1,0:T(8,128)(2,1)S(1)} %bitcast.29), channel_id=1, source_target_pairs={{0,128},{64,192},{128,0},{192,64},{1,129},{65,193},{129,1},{193,65... | collective-permute-start | bytes 786440 | tf_op jit(solution)/shard_map/ppermute | solution.py:343
  70.6 6.2 %count_matrix.3 = bf16[2048,2048]{1,0:T(8,128)(2,1)S(1)} custom-call(s32[8,2048]{1,0:T(8,128)S(1)} %get-tuple-element.24.nbrs_ref, s32[1,2048]{1,0:T(1,128)S(1)} %get-tuple-element.25.count_ref), custom_call_target="tpu_custom_call" | custom-call | flops 6710886400 | bytes 8388608 | tf_op jit(solution)/shard_map/count_matrix/pallas_call | solution.py:166
  76.9 1.6 %count_matrix.5.mat_ref = bf16[512,2048]{1,0:T(8,128)(2,1)S(1)} custom-call(s32[8,2048]{1,0:T(8,128)S(1)} %get-tuple-element.24.nbrs_ref, s32[1,2048]{1,0:T(1,128)S(1)} %get-tuple-element.25.count_ref), custom_call_target="tpu_custom_call" | custom-call | flops 1677721600 | bytes 2097152 | tf_op jit(solution)/shard_map/count_matrix/pallas_call | solution.py:166
  79.9 7.8 %collective-permute-start.9 = (bf16[256,512]{1,0:T(8,128)(2,1)S(1)}, bf16[256,512]{1,0:T(8,128)(2,1)S(1)}, u32[]{:S(2)}, u32[]{:S(2)}) collective-permute-start(bf16[256,512]{1,0:T(8,128)(2,1)S(1)} %convolution_convert_fusion), channel_id=1, source_target_pairs={{0,1},{1,2},{2,3},{3,4},{4,5},{5,6},{6,7},{7,0},{8,9},{9,10},{10,1... | collective-permute-start | bytes 786440 | tf_op jit(solution)/shard_map/ppermute | solution.py:343
  87.7 2.3 %fusion.15.total_ref = f32[256,2048]{1,0:T(8,128)S(1)} fusion(bf16[256,2048]{1,0:T(8,128)(2,1)S(1)} %fusion.3.hidden_ref, bf16[2048,2048]{1,0:T(8,128)(2,1)S(1)} %count_matrix.3), kind=kOutput, calls=%fused_computation.31 | convolution fusion | flops 2147483648 | bytes 11534336 | tf_op jit(solution)/shard_map/dot_general | solution.py:19
  91.1 8.1 %mlp.1 = (bf16[256,512]{1,0:T(8,128)(2,1)S(1)}, f32[256,2048]{1,0:T(8,128)S(1)}, bf16[256,2048]{1,0:T(8,128)(2,1)S(1)}, bf16[256,512]{1,0:T(8,128)(2,1)S(1)}) custom-call(f32[256,2048]{1,0:T(8,128)S(1)} %fusion.15.total_ref, bf16[256,512]{1,0:T(8,128)(2,1)S(1)} %collective-permute-done.9.received_ref, bf16[512,2048]{1,0:T(8,128)(2,1)S(1)} %count_matrix.5.mat_ref, ...), custom_call_target="tpu_custom_call" | custom-call | flops 3221225472 | bytes 20971520 | tf_op jit(solution)/shard_map/mlp/pallas_call | solution.py:278
  99.1 2.6 %collective-permute-start.17 = (bf16[256,512]{1,0:T(8,128)(2,1)S(1)}, bf16[256,512]{1,0:T(8,128)(2,1)S(1)}, u32[]{:S(2)}, u32[]{:S(2)}) collective-permute-start(bf16[256,512]{1,0:T(8,128)(2,1)S(1)} %get-tuple-element.28), channel_id=1, source_target_pairs={{0,7},{1,0},{2,1},{3,2},{4,3},{5,4},{6,5},{7,6},{8,15},{9,8},{10,9... | collective-permute-start | bytes 786440 | tf_op jit(solution)/shard_map/ppermute | solution.py:343
  101.8 2.4 %fusion.16 = f32[256,2048]{1,0:T(8,128)S(1)} fusion(bf16[256,2048]{1,0:T(8,128)(2,1)S(1)} %get-tuple-element.27, bf16[2048,2048]{1,0:T(8,128)(2,1)S(1)} %count_matrix.3), kind=kOutput, calls=%fused_computation.32 | convolution fusion | flops 2147483648 | bytes 11534336 | tf_op jit(solution)/shard_map/dot_general | solution.py:23
  104.5 1.2 collective-permute-done.17.returned_ref
  105.7 2.0 %last.1 = (f32[160,256]{1,0:T(8,128)S(1)}, f32[160,256]{1,0:T(8,128)}) custom-call(s32[1]{0:T(128)} %bitcast.core_ref, f32[256,2048]{1,0:T(8,128)S(1)} %add.63.part_ref, bf16[256,512]{1,0:T(8,128)(2,1)S(1)} %collective-permute-done.17.returned_ref, bf16[2048,512]{1,0:T(8,128)(2,1)S(1)} %count_matrix.4.pick_ref, bf16[256,512]{1,0:T(8,128)(2,1)S(1)} %bitcast.32, ...), custom_call_target="tpu_custom_call" | custom-call | flops 4294967296 | bytes 8388608 | tf_op jit(solution)/shard_map/last/pallas_call | solution.py:334
  108.5 1.6 %collective-permute-done.18 = f32[160,256]{1,0:T(8,128)S(1)} collective-permute-done((f32[160,256]{1,0:T(8,128)}, f32[160,256]{1,0:T(8,128)S(1)}, u32[]{:S(2)}, u32[]{:S(2)}) %collective-permute-start.18) | collective-permute-done | bytes 163872 | tf_op jit(solution)/shard_map/ppermute | solution.py:347
  111.0 1.3 %collective-permute-start.19 = (bf16[160,256]{1,0:T(8,128)(2,1)S(1)}, bf16[160,256]{1,0:T(8,128)(2,1)S(1)}, u32[]{:S(2)}, u32[]{:S(2)}) collective-permute-start(bf16[160,256]{1,0:T(8,128)(2,1)S(1)} %add_convert_fusion.1), channel_id=1, source_target_pairs={{0,2},{2,0},{4,6},{6,4},{1,3},{3,1},{5,7},{7,5},{8,10},{10,8},{12,... | collective-permute-start | bytes 245768 | tf_op jit(solution)/shard_map/ppermute | solution.py:347
  112.3 2.7 %collective-permute-start.20 = (bf16[160,256]{1,0:T(8,128)(2,1)S(1)}, bf16[160,256]{1,0:T(8,128)(2,1)S(1)}, u32[]{:S(2)}, u32[]{:S(2)}) collective-permute-start(bf16[160,256]{1,0:T(8,128)(2,1)S(1)} %add_convert_fusion.1), channel_id=1, source_target_pairs={{0,4},{2,6},{4,0},{6,2},{1,5},{3,7},{5,1},{7,3},{8,12},{10,14},{12... | collective-permute-start | bytes 245768 | tf_op jit(solution)/shard_map/ppermute | solution.py:347
  114.9 1.8 %fusion.4 = bf16[64,256]{0,1:T(8,128)(2,1)S(1)} fusion(bf16[1024,256]{1,0:T(8,128)(2,1)} %w_out_ref.1, bf16[256,1024]{1,0:T(8,128)(2,1)} %w_in_ref.1, bf16[256,512]{1,0:T(8,128)(2,1)} %copy-done.8, s32[]{:T(128)S(6)} %select_n.64, bf16[256,2048]{1,0:T(8,128)(2,1)S(1)} %fusion.3.hidden_ref, s32[]{:T(128)S(6)} %select_n.63), kind=kOutput, calls=%fused_computation.8 | convolution fusion | flops 67485696 | bytes 1179656 | tf_op jit(solution)/shard_map/dot_general | solution.py:19
  116.8 2.3 %collective-permute-done.20 = bf16[160,256]{1,0:T(8,128)(2,1)S(1)} collective-permute-done((bf16[160,256]{1,0:T(8,128)(2,1)S(1)}, bf16[160,256]{1,0:T(8,128)(2,1)S(1)}, u32[]{:S(2)}, u32[]{:S(2)}) %collective-permute-start.20) | collective-permute-done | bytes 81952 | tf_op jit(solution)/shard_map/ppermute | solution.py:347
  119.1 2.0 %collective-permute-done.21 = bf16[160,256]{1,0:T(8,128)(2,1)S(1)} collective-permute-done((bf16[160,256]{1,0:T(8,128)(2,1)S(1)}, bf16[160,256]{1,0:T(8,128)(2,1)S(1)}, u32[]{:S(2)}, u32[]{:S(2)}) %collective-permute-start.21) | collective-permute-done | bytes 81952 | tf_op jit(solution)/shard_map/ppermute | solution.py:347
  (88 shorter events, 16.8 us)
Async XLA Ops:
  8.9 26.7 %collective-permute-start.1 = (bf16[256,512]{1,0:T(8,128)(2,1)}, bf16[256,512]{1,0:T(8,128)(2,1)S(1)}, u32[]{:S(2)}, u32[]{:S(2)}) collective-permute-start(bf16[256,512]{1,0:T(8,128)(2,1)} %get-tuple-element.21), channel_id=1, source_target_pairs={{0,64},{64,128},{128,192},{192,0},{1,65},{65,129},{129,193},{193,1... | collective-permute-start | bytes 786440 | tf_op jit(solution)/shard_map/ppermute | solution.py:343
  11.1 24.5 %collective-permute-start.2 = (bf16[256,512]{1,0:T(8,128)(2,1)}, bf16[256,512]{1,0:T(8,128)(2,1)S(1)}, u32[]{:S(2)}, u32[]{:S(2)}) collective-permute-start(bf16[256,512]{1,0:T(8,128)(2,1)} %get-tuple-element.22), channel_id=1, source_target_pairs={{0,192},{64,0},{128,64},{192,128},{1,193},{65,1},{129,65},{193,129... | collective-permute-start | bytes 786440 | tf_op jit(solution)/shard_map/ppermute | solution.py:343
  18.2 9.9 %copy-start.5 = (s32[64,8]{0,1:T(8,128)S(1)}, s32[64,8]{0,1:T(8,128)}, u32[]{:S(2)}) copy-start(s32[64,8]{0,1:T(8,128)} %param.17) | copy-start | bytes 6148
  18.2 9.9 %copy-start.15 = (f32[256]{0:T(256)S(1)}, f32[256]{0:T(256)}, u32[]{:S(2)}) copy-start(f32[256]{0:T(256)} %param.15) | copy-start | bytes 3076
  18.2 17.3 %collective-permute-start = (bf16[256,512]{1,0:T(8,128)(2,1)}, bf16[256,512]{1,0:T(8,128)(2,1)S(1)}, u32[]{:S(2)}, u32[]{:S(2)}) collective-permute-start(bf16[256,512]{1,0:T(8,128)(2,1)} %get-tuple-element.20), channel_id=1, source_target_pairs={{0,128},{64,192},{128,0},{192,64},{1,129},{65,193},{129,1},{193,65... | collective-permute-start | bytes 786440 | tf_op jit(solution)/shard_map/ppermute | solution.py:343
  19.9 8.4 %collective-permute-start.10 = (bf16[64,256]{1,0:T(8,128)(2,1)S(1)}, bf16[64,256]{1,0:T(8,128)(2,1)S(1)}, u32[]{:S(2)}, u32[]{:S(2)}) collective-permute-start(bf16[64,256]{1,0:T(8,128)(2,1)S(1)} %copy-done.13), channel_id=1, source_target_pairs={{0,8},{8,0},{16,24},{24,16},{32,40},{40,32},{48,56},{56,48},{1,9},... | collective-permute-start | bytes 98312 | tf_op jit(solution)/shard_map/ppermute | solution.py:347
  28.2 15.0 %collective-permute-start.11 = (bf16[128,256]{1,0:T(8,128)(2,1)S(1)}, bf16[128,256]{1,0:T(8,128)(2,1)S(1)}, u32[]{:S(2)}, u32[]{:S(2)}) collective-permute-start(bf16[128,256]{1,0:T(8,128)(2,1)S(1)} %maximum_select_fusion.1), channel_id=1, source_target_pairs={{0,16},{8,24},{16,0},{24,8},{32,48},{40,56},{48,32},{56,40},{1,17}... | collective-permute-start | bytes 196616 | tf_op jit(solution)/shard_map/ppermute | solution.py:347
  31.3 11.9 %collective-permute-start.12 = (bf16[128,256]{1,0:T(8,128)(2,1)S(1)}, bf16[128,256]{1,0:T(8,128)(2,1)S(1)}, u32[]{:S(2)}, u32[]{:S(2)}) collective-permute-start(bf16[128,256]{1,0:T(8,128)(2,1)S(1)} %maximum_select_fusion.1), channel_id=1, source_target_pairs={{0,32},{8,40},{16,48},{24,56},{32,0},{40,8},{48,16},{56,24},{1,33}... | collective-permute-start | bytes 196616 | tf_op jit(solution)/shard_map/ppermute | solution.py:347
  35.5 7.7 %collective-permute-start.13 = (bf16[128,256]{1,0:T(8,128)(2,1)S(1)}, bf16[128,256]{1,0:T(8,128)(2,1)S(1)}, u32[]{:S(2)}, u32[]{:S(2)}) collective-permute-start(bf16[128,256]{1,0:T(8,128)(2,1)S(1)} %maximum_select_fusion.1), channel_id=1, source_target_pairs={{0,48},{8,56},{16,32},{24,40},{32,16},{40,24},{48,0},{56,8},{1,49}... | collective-permute-start | bytes 196616 | tf_op jit(solution)/shard_map/ppermute | solution.py:347
  36.7 22.2 %copy-start.14 = (s32[512]{0:T(512)S(1)}, s32[512]{0:T(512)}, u32[]{:S(2)}) copy-start(s32[512]{0:T(512)} %param.16) | copy-start | bytes 6148
  37.4 17.1 %all-to-all-start = ((bf16[8,48,512]{2,1,0:T(8,128)(2,1)}), bf16[8,48,512]{2,1,0:T(8,128)(2,1)S(1)}, u32[]{:S(2)}, u32[]{:S(2)}) async-start(bf16[8,48,512]{2,1,0:T(8,128)(2,1)} %pad_maximum_fusion.1), calls=%async_computation | async-start | bytes 786432 | tf_op jit(solution)/shard_map/all_to_all | solution.py:400
  43.4 18.2 %collective-permute-start.14 = (bf16[512,256]{1,0:T(8,128)(2,1)S(1)}, bf16[512,256]{1,0:T(8,128)(2,1)S(1)}, u32[]{:S(2)}, u32[]{:S(2)}) collective-permute-start(bf16[512,256]{1,0:T(8,128)(2,1)S(1)} %bitcast.39), channel_id=1, source_target_pairs={{0,192},{64,0},{128,64},{192,128},{1,193},{65,1},{129,65},{193,129... | collective-permute-start | bytes 786440 | tf_op jit(solution)/shard_map/ppermute | solution.py:343
  44.3 17.7 %collective-permute-start.15 = (bf16[512,256]{1,0:T(8,128)(2,1)S(1)}, bf16[512,256]{1,0:T(8,128)(2,1)}, u32[]{:S(2)}, u32[]{:S(2)}) collective-permute-start(bf16[512,256]{1,0:T(8,128)(2,1)S(1)} %bitcast.40), channel_id=1, source_target_pairs={{0,128},{64,192},{128,0},{192,64},{1,129},{65,193},{129,1},{193,65... | collective-permute-start | bytes 786440 | tf_op jit(solution)/shard_map/ppermute | solution.py:343
  45.7 16.3 %collective-permute-start.16 = (bf16[512,256]{1,0:T(8,128)(2,1)S(1)}, bf16[512,256]{1,0:T(8,128)(2,1)}, u32[]{:S(2)}, u32[]{:S(2)}) collective-permute-start(bf16[512,256]{1,0:T(8,128)(2,1)S(1)} %bitcast.41), channel_id=1, source_target_pairs={{0,64},{64,128},{128,192},{192,0},{1,65},{65,129},{129,193},{193,1... | collective-permute-start | bytes 786440 | tf_op jit(solution)/shard_map/ppermute | solution.py:343
  55.4 12.7 %all-to-all-start.1 = ((bf16[8,32,512]{2,1,0:T(8,128)(2,1)}), bf16[8,32,512]{2,1,0:T(8,128)(2,1)S(1)}, u32[]{:S(2)}, u32[]{:S(2)}) async-start(bf16[8,32,512]{2,1,0:T(8,128)(2,1)} %broadcast_in_dim.28), calls=%async_computation.1 | async-start | bytes 524288 | tf_op jit(solution)/shard_map/all_to_all | solution.py:352
  59.3 4.8 %collective-permute-start.6 = (bf16[8,16,256]{2,1,0:T(8,128)(2,1)S(1)}, bf16[8,16,256]{2,1,0:T(8,128)(2,1)S(1)}, u32[]{:S(2)}, u32[]{:S(2)}) collective-permute-start(bf16[8,16,256]{2,1,0:T(8,128)(2,1)S(1)} %slice.9.refs_0_), channel_id=1, source_target_pairs={{0,192},{64,0},{128,64},{192,128},{1,193},{65,1},{129,65},{193,129... | collective-permute-start | bytes 196616 | tf_op jit(solution)/shard_map/ppermute | solution.py:343
  60.2 4.6 %collective-permute-start.7 = (bf16[8,16,256]{2,1,0:T(8,128)(2,1)S(1)}, bf16[8,16,256]{2,1,0:T(8,128)(2,1)S(1)}, u32[]{:S(2)}, u32[]{:S(2)}) collective-permute-start(bf16[8,16,256]{2,1,0:T(8,128)(2,1)S(1)} %slice.9.refs_0_), channel_id=1, source_target_pairs={{0,128},{64,192},{128,0},{192,64},{1,129},{65,193},{129,1},{193,65... | collective-permute-start | bytes 196616 | tf_op jit(solution)/shard_map/ppermute | solution.py:343
  61.6 4.3 %collective-permute-start.8 = (bf16[8,16,256]{2,1,0:T(8,128)(2,1)S(1)}, bf16[8,16,256]{2,1,0:T(8,128)(2,1)S(1)}, u32[]{:S(2)}, u32[]{:S(2)}) collective-permute-start(bf16[8,16,256]{2,1,0:T(8,128)(2,1)S(1)} %slice.9.refs_0_), channel_id=1, source_target_pairs={{0,64},{64,128},{128,192},{192,0},{1,65},{65,129},{129,193},{193,1... | collective-permute-start | bytes 196616 | tf_op jit(solution)/shard_map/ppermute | solution.py:343
  68.1 10.4 %collective-permute-start.3 = (bf16[256,512]{1,0:T(8,128)(2,1)S(1)}, bf16[256,512]{1,0:T(8,128)(2,1)S(1)}, u32[]{:S(2)}, u32[]{:S(2)}) collective-permute-start(bf16[256,512]{1,0:T(8,128)(2,1)S(1)} %bitcast.28), channel_id=1, source_target_pairs={{0,192},{64,0},{128,64},{192,128},{1,193},{65,1},{129,65},{193,129... | collective-permute-start | bytes 786440 | tf_op jit(solution)/shard_map/ppermute | solution.py:343
  68.9 9.6 %collective-permute-start.4 = (bf16[256,512]{1,0:T(8,128)(2,1)S(1)}, bf16[256,512]{1,0:T(8,128)(2,1)S(1)}, u32[]{:S(2)}, u32[]{:S(2)}) collective-permute-start(bf16[256,512]{1,0:T(8,128)(2,1)S(1)} %bitcast.29), channel_id=1, source_target_pairs={{0,128},{64,192},{128,0},{192,64},{1,129},{65,193},{129,1},{193,65... | collective-permute-start | bytes 786440 | tf_op jit(solution)/shard_map/ppermute | solution.py:343
  70.3 8.2 %collective-permute-start.5 = (bf16[256,512]{1,0:T(8,128)(2,1)S(1)}, bf16[256,512]{1,0:T(8,128)(2,1)S(1)}, u32[]{:S(2)}, u32[]{:S(2)}) collective-permute-start(bf16[256,512]{1,0:T(8,128)(2,1)S(1)} %bitcast.30), channel_id=1, source_target_pairs={{0,64},{64,128},{128,192},{192,0},{1,65},{65,129},{129,193},{193,1... | collective-permute-start | bytes 786440 | tf_op jit(solution)/shard_map/ppermute | solution.py:343
  79.8 11.2 %copy-start = (bf16[2048,256]{1,0:T(8,128)(2,1)S(1)}, bf16[2048,256]{1,0:T(8,128)(2,1)}, u32[]{:S(2)}) copy-start(bf16[2048,256]{1,0:T(8,128)(2,1)} %pad_maximum_fusion.cot_ref) | copy-start | bytes 3145732
  79.8 11.2 %copy-start.2 = (bf16[256,1024]{1,0:T(8,128)(2,1)S(1)}, bf16[256,1024]{1,0:T(8,128)(2,1)}, u32[]{:S(2)}) copy-start(bf16[256,1024]{1,0:T(8,128)(2,1)} %w_in_ref.1) | copy-start | bytes 1572868
  79.8 11.2 %copy-start.3 = (bf16[256,1024]{0,1:T(8,128)(2,1)S(1)}, bf16[256,1024]{0,1:T(8,128)(2,1)}, u32[]{:S(2)}) copy-start(bf16[256,1024]{0,1:T(8,128)(2,1)} %copy.13) | copy-start | bytes 1572868
  79.9 11.2 %copy-start.7 = (bf16[1024,256]{1,0:T(8,128)(2,1)S(1)}, bf16[1024,256]{1,0:T(8,128)(2,1)}, u32[]{:S(2)}) copy-start(bf16[1024,256]{1,0:T(8,128)(2,1)} %w_out_ref.1) | copy-start | bytes 1572868
  79.9 11.2 %collective-permute-start.9 = (bf16[256,512]{1,0:T(8,128)(2,1)S(1)}, bf16[256,512]{1,0:T(8,128)(2,1)S(1)}, u32[]{:S(2)}, u32[]{:S(2)}) collective-permute-start(bf16[256,512]{1,0:T(8,128)(2,1)S(1)} %convolution_convert_fusion), channel_id=1, source_target_pairs={{0,1},{1,2},{2,3},{3,4},{4,5},{5,6},{6,7},{7,0},{8,9},{9,10},{10,1... | collective-permute-start | bytes 786440 | tf_op jit(solution)/shard_map/ppermute | solution.py:343
  99.1 6.6 %collective-permute-start.17 = (bf16[256,512]{1,0:T(8,128)(2,1)S(1)}, bf16[256,512]{1,0:T(8,128)(2,1)S(1)}, u32[]{:S(2)}, u32[]{:S(2)}) collective-permute-start(bf16[256,512]{1,0:T(8,128)(2,1)S(1)} %get-tuple-element.28), channel_id=1, source_target_pairs={{0,7},{1,0},{2,1},{3,2},{4,3},{5,4},{6,5},{7,6},{8,15},{9,8},{10,9... | collective-permute-start | bytes 786440 | tf_op jit(solution)/shard_map/ppermute | solution.py:343
  108.4 1.6 %collective-permute-start.18 = (f32[160,256]{1,0:T(8,128)}, f32[160,256]{1,0:T(8,128)S(1)}, u32[]{:S(2)}, u32[]{:S(2)}) collective-permute-start(f32[160,256]{1,0:T(8,128)} %get-tuple-element.34), channel_id=1, source_target_pairs={{0,1},{1,0},{2,3},{3,2},{4,5},{5,4},{6,7},{7,6},{8,9},{9,8},{10,11... | collective-permute-start | bytes 491528 | tf_op jit(solution)/shard_map/ppermute | solution.py:347
  111.0 5.8 %collective-permute-start.19 = (bf16[160,256]{1,0:T(8,128)(2,1)S(1)}, bf16[160,256]{1,0:T(8,128)(2,1)S(1)}, u32[]{:S(2)}, u32[]{:S(2)}) collective-permute-start(bf16[160,256]{1,0:T(8,128)(2,1)S(1)} %add_convert_fusion.1), channel_id=1, source_target_pairs={{0,2},{2,0},{4,6},{6,4},{1,3},{3,1},{5,7},{7,5},{8,10},{10,8},{12,... | collective-permute-start | bytes 245768 | tf_op jit(solution)/shard_map/ppermute | solution.py:347
  112.3 6.8 %collective-permute-start.20 = (bf16[160,256]{1,0:T(8,128)(2,1)S(1)}, bf16[160,256]{1,0:T(8,128)(2,1)S(1)}, u32[]{:S(2)}, u32[]{:S(2)}) collective-permute-start(bf16[160,256]{1,0:T(8,128)(2,1)S(1)} %add_convert_fusion.1), channel_id=1, source_target_pairs={{0,4},{2,6},{4,0},{6,2},{1,5},{3,7},{5,1},{7,3},{8,12},{10,14},{12... | collective-permute-start | bytes 245768 | tf_op jit(solution)/shard_map/ppermute | solution.py:347
  114.9 6.2 %collective-permute-start.21 = (bf16[160,256]{1,0:T(8,128)(2,1)S(1)}, bf16[160,256]{1,0:T(8,128)(2,1)S(1)}, u32[]{:S(2)}, u32[]{:S(2)}) collective-permute-start(bf16[160,256]{1,0:T(8,128)(2,1)S(1)} %add_convert_fusion.1), channel_id=1, source_target_pairs={{0,6},{2,4},{4,2},{6,0},{1,7},{3,5},{5,3},{7,1},{8,14},{10,12},{12... | collective-permute-start | bytes 245768 | tf_op jit(solution)/shard_map/ppermute | solution.py:347
  121.2 1.8 %collective-permute-start.22 = (f32[160,256]{1,0:T(8,128)S(1)}, f32[160,256]{1,0:T(8,128)S(1)}, u32[]{:S(2)}, u32[]{:S(2)}) collective-permute-start(f32[160,256]{1,0:T(8,128)S(1)} %add_add_fusion), channel_id=1, source_target_pairs={{0,1},{1,0},{2,3},{3,2},{4,5},{5,4},{6,7},{7,6},{8,9},{9,8},{10,11... | collective-permute-start | bytes 491528 | tf_op jit(solution)/shard_map/ppermute | solution.py:347
  (9 other events, 39.4 us)

commit v3 on v2

--- a/solution.py
+++ b/solution.py
@@ -91,7 +91,7 @@
     part_ref[...] = dot_tn(w, agg).astype(BF)
 
 
-PIECES = 4
+PIECES = 8
 
 
 def chunk_body(y_ref, face_hbm, nbrs_hbm, count_hbm, w_hbm, *refs, group):
@@ -430,7 +430,10 @@
 
     keep, give = last(core.reshape(1), grad_part, returned, pick, pre, [agg[d] for d in range(NY)])
     pair = (keep + swap(give, "core", 1)).astype(BF)
-    one, two, three = (swap(pair, "x", bit).astype(F32) for bit in (1, 2, 3))
+    others = []
+    for bit in (1, 2, 3):
+        others.append(swap(pair, "x", bit))
+    one, two, three = (other.astype(F32) for other in others)
     done = (pair.astype(F32) + one) + (two + three)
     done, embed = lax.optimization_barrier((done, embed))
     other = swap(done, "core", 1)

time: 124 us -> 124 us (level)
  the two profiles are of different devices: /device:TPU:1 before, /device:TPU:8 now
where the time goes in v3:
time: 124 us; the launch traced here: 122 us
  starting transfers between devices  41.1 us (33%)
  Pallas kernels  38.2 us (31%)
  waiting for transfers between devices  24.1 us (19%)
  matrix products  7.19 us (6%)
  other arithmetic  6.95 us (6%)
  local copies, waits for them, and re-layouts  3.3 us (3%)
    pallas_call x3, Pallas kernels, agg_chunk(): pl.pallas_call(functools.partial(chunk_body, group=group), grid_spec=spec...  19.6 us
    ppermute x14, starting transfers between devices, shift(): lax.ppermute(value, axis, [(i, (i + by) % devices) for i in range(devices)])  16.2 us
    ppermute x9, starting transfers between devices, swap(): lax.ppermute(value, axis, [(i, i ^ bit) for i in range(lax.axis_size(axis...  15.2 us
    all_to_all x1, waiting for transfers between devices, body(): by_z = lax.all_to_all(part_y, 'z', 0, 0)  8.59 us
    pallas_call x3, Pallas kernels, count_matrix(): pl.pallas_call(functools.partial(count_body, first=first), grid=(rows //...  8.21 us
    pallas_call x1, Pallas kernels, mlp(): pl.pallas_call(mlp_body, grid=(NY,), in_specs=[tile, whole((hid, halo)),...  8.09 us
    ppermute x14, waiting for transfers between devices, shift(): lax.ppermute(value, axis, [(i, (i + by) % devices) for i in range(devices)])  6.95 us
    all_to_all x1, starting transfers between devices, body(): by_z = lax.all_to_all(part_y, 'z', 0, 0)  6.29 us
  transfers between devices with their start and end apart: 25, of which 9 were waited for; matrix products, arithmetic and copies ran while one was open for 11% of the time, Pallas kernels for 16%

profile of v3, /device:TPU:8, one launch (start us, length us, event | category | flops | bytes accessed | tf_op | source)
XLA Modules:
  0.0 122.0 jit_solution(16868689185588562058)
XLA Ops:
  0.6 8.4 %agg_chunk.4 = (bf16[320,512]{1,0:T(8,128)(2,1)}, bf16[256,512]{1,0:T(8,128)(2,1)}, bf16[320,512]{1,0:T(8,128)(2,1)}, bf16[256,512]{1,0:T(8,128)(2,1)}) custom-call(s32[1]{0:T(128)} %bitcast.1.y_ref, bf16[320,4096]{1,0:T(8,128)(2,1)} %bitcast.48, s32[8,2048]{1,0:T(8,128)} %bitcast.51, s32[1,2048]{1,0:T(1,128)} %bitcast.54, bf16[320,256]{1,0:T(8,128)(2,1)} %w_hbm.5), custom_call_target="tpu_custom_call" | custom-call | flops 2852126720 | bytes 4194304 | tf_op jit(solution)/shard_map/agg_chunk/pallas_call | solution.py:141
  9.0 1.6 %collective-permute-start.1 = (bf16[256,512]{1,0:T(8,128)(2,1)}, bf16[256,512]{1,0:T(8,128)(2,1)S(1)}, u32[]{:S(2)}, u32[]{:S(2)}) collective-permute-start(bf16[256,512]{1,0:T(8,128)(2,1)} %get-tuple-element.21), channel_id=1, source_target_pairs={{0,64},{64,128},{128,192},{192,0},{1,65},{65,129},{129,193},{193,1... | collective-permute-start | bytes 786440 | tf_op jit(solution)/shard_map/ppermute | solution.py:343
  11.4 5.6 %agg_chunk.3 = (bf16[320,512]{1,0:T(8,128)(2,1)}, bf16[256,512]{1,0:T(8,128)(2,1)}) custom-call(s32[1]{0:T(128)} %bitcast.1.y_ref, bf16[320,4096]{1,0:T(8,128)(2,1)} %bitcast.49, s32[8,2048]{1,0:T(8,128)} %bitcast.52, s32[1,2048]{1,0:T(1,128)} %bitcast.55, bf16[320,256]{1,0:T(8,128)(2,1)} %w_hbm.5), custom_call_target="tpu_custom_call" | custom-call | flops 1426063360 | bytes 4194304 | tf_op jit(solution)/shard_map/agg_chunk/pallas_call | solution.py:141
  17.0 2.2 %collective-permute-start = (bf16[256,512]{1,0:T(8,128)(2,1)}, bf16[256,512]{1,0:T(8,128)(2,1)S(1)}, u32[]{:S(2)}, u32[]{:S(2)}) collective-permute-start(bf16[256,512]{1,0:T(8,128)(2,1)} %get-tuple-element.20), channel_id=1, source_target_pairs={{0,128},{64,192},{128,0},{192,64},{1,129},{65,193},{129,1},{193,65... | collective-permute-start | bytes 786440 | tf_op jit(solution)/shard_map/ppermute | solution.py:343
  19.2 1.9 %collective-permute-start.10 = (bf16[64,256]{1,0:T(8,128)(2,1)S(1)}, bf16[64,256]{1,0:T(8,128)(2,1)S(1)}, u32[]{:S(2)}, u32[]{:S(2)}) collective-permute-start(bf16[64,256]{1,0:T(8,128)(2,1)S(1)} %copy-done.13), channel_id=1, source_target_pairs={{0,8},{8,0},{16,24},{24,16},{32,40},{40,32},{48,56},{56,48},{1,9},... | collective-permute-start | bytes 98312 | tf_op jit(solution)/shard_map/ppermute | solution.py:347
  21.1 5.6 %agg_chunk.5 = (bf16[320,512]{1,0:T(8,128)(2,1)}, bf16[256,512]{1,0:T(8,128)(2,1)}) custom-call(s32[1]{0:T(128)} %bitcast.1.y_ref, bf16[320,4096]{1,0:T(8,128)(2,1)} %bitcast.50, s32[8,2048]{1,0:T(8,128)} %bitcast.53, s32[1,2048]{1,0:T(1,128)} %bitcast.56, bf16[320,256]{1,0:T(8,128)(2,1)} %w_hbm.5), custom_call_target="tpu_custom_call" | custom-call | flops 1426063360 | bytes 4194304 | tf_op jit(solution)/shard_map/agg_chunk/pallas_call | solution.py:141
  27.9 3.4 %collective-permute-start.11 = (bf16[128,256]{1,0:T(8,128)(2,1)S(1)}, bf16[128,256]{1,0:T(8,128)(2,1)S(1)}, u32[]{:S(2)}, u32[]{:S(2)}) collective-permute-start(bf16[128,256]{1,0:T(8,128)(2,1)S(1)} %maximum_select_fusion.1), channel_id=1, source_target_pairs={{0,16},{8,24},{16,0},{24,8},{32,48},{40,56},{48,32},{56,40},{1,17}... | collective-permute-start | bytes 196616 | tf_op jit(solution)/shard_map/ppermute | solution.py:347
  31.3 4.5 %collective-permute-start.12 = (bf16[128,256]{1,0:T(8,128)(2,1)S(1)}, bf16[128,256]{1,0:T(8,128)(2,1)S(1)}, u32[]{:S(2)}, u32[]{:S(2)}) collective-permute-start(bf16[128,256]{1,0:T(8,128)(2,1)S(1)} %maximum_select_fusion.1), channel_id=1, source_target_pairs={{0,32},{8,40},{16,48},{24,56},{32,0},{40,8},{48,16},{56,24},{1,33}... | collective-permute-start | bytes 196616 | tf_op jit(solution)/shard_map/ppermute | solution.py:347
  37.7 6.3 %all-to-all-start = ((bf16[8,48,512]{2,1,0:T(8,128)(2,1)}), bf16[8,48,512]{2,1,0:T(8,128)(2,1)S(1)}, u32[]{:S(2)}, u32[]{:S(2)}) async-start(bf16[8,48,512]{2,1,0:T(8,128)(2,1)} %pad_maximum_fusion.1), calls=%async_computation | async-start | bytes 786432 | tf_op jit(solution)/shard_map/all_to_all | solution.py:400
  44.2 1.4 %collective-permute-start.14 = (bf16[512,256]{1,0:T(8,128)(2,1)S(1)}, bf16[512,256]{1,0:T(8,128)(2,1)S(1)}, u32[]{:S(2)}, u32[]{:S(2)}) collective-permute-start(bf16[512,256]{1,0:T(8,128)(2,1)S(1)} %bitcast.39), channel_id=1, source_target_pairs={{0,192},{64,0},{128,64},{192,128},{1,193},{65,1},{129,65},{193,129... | collective-permute-start | bytes 786440 | tf_op jit(solution)/shard_map/ppermute | solution.py:343
  46.6 1.6 %collective-permute-start.16 = (bf16[512,256]{1,0:T(8,128)(2,1)S(1)}, bf16[512,256]{1,0:T(8,128)(2,1)}, u32[]{:S(2)}, u32[]{:S(2)}) collective-permute-start(bf16[512,256]{1,0:T(8,128)(2,1)S(1)} %bitcast.41), channel_id=1, source_target_pairs={{0,64},{64,128},{128,192},{192,0},{1,65},{65,129},{129,193},{193,1... | collective-permute-start | bytes 786440 | tf_op jit(solution)/shard_map/ppermute | solution.py:343
  48.2 8.6 %all-to-all-done = bf16[8,48,512]{2,1,0:T(8,128)(2,1)S(1)} async-done(((bf16[8,48,512]{2,1,0:T(8,128)(2,1)}), bf16[8,48,512]{2,1,0:T(8,128)(2,1)S(1)}, u32[]{:S(2)}, u32[]{:S(2)}) %all-to-all-start) | async-done | bytes 393248 | tf_op jit(solution)/shard_map/all_to_all | solution.py:400
  57.6 3.4 %all-to-all-start.1 = ((bf16[8,32,512]{2,1,0:T(8,128)(2,1)}), bf16[8,32,512]{2,1,0:T(8,128)(2,1)S(1)}, u32[]{:S(2)}, u32[]{:S(2)}) async-start(bf16[8,32,512]{2,1,0:T(8,128)(2,1)} %broadcast_in_dim.28), calls=%async_computation.1 | async-start | bytes 524288 | tf_op jit(solution)/shard_map/all_to_all | solution.py:352
  61.5 1.4 %collective-permute-start.6 = (bf16[8,16,256]{2,1,0:T(8,128)(2,1)S(1)}, bf16[8,16,256]{2,1,0:T(8,128)(2,1)S(1)}, u32[]{:S(2)}, u32[]{:S(2)}) collective-permute-start(bf16[8,16,256]{2,1,0:T(8,128)(2,1)S(1)} %slice.9.refs_0_), channel_id=1, source_target_pairs={{0,192},{64,0},{128,64},{192,128},{1,193},{65,1},{129,65},{193,129... | collective-permute-start | bytes 196616 | tf_op jit(solution)/shard_map/ppermute | solution.py:343
  64.0 1.4 %collective-permute-start.8 = (bf16[8,16,256]{2,1,0:T(8,128)(2,1)S(1)}, bf16[8,16,256]{2,1,0:T(8,128)(2,1)S(1)}, u32[]{:S(2)}, u32[]{:S(2)}) collective-permute-start(bf16[8,16,256]{2,1,0:T(8,128)(2,1)S(1)} %slice.9.refs_0_), channel_id=1, source_target_pairs={{0,64},{64,128},{128,192},{192,0},{1,65},{65,129},{129,193},{193,1... | collective-permute-start | bytes 196616 | tf_op jit(solution)/shard_map/ppermute | solution.py:343
  65.4 2.1 %pad_maximum_fusion.cot_ref = bf16[2048,256]{1,0:T(8,128)(2,1)} fusion(bf16[512,256]{1,0:T(8,128)(2,1)} %collective-permute-done.16, bf16[512,256]{1,0:T(8,128)(2,1)} %collective-permute-done.15, bf16[512,256]{1,0:T(8,128)(2,1)S(1)} %collective-permute-done.14, bf16[512,256]{1,0:T(8,128)(2,1)S(1)} %bitcast.42), kind=kLoop, calls=%fused_computation.9 | loop fusion | flops 4194304 | bytes 2097152 | tf_op jit(solution)/shard_map/concatenate | solution.py:412
  68.8 2.6 %all-to-all-done.1 = bf16[8,32,512]{2,1,0:T(8,128)(2,1)S(1)} async-done(((bf16[8,32,512]{2,1,0:T(8,128)(2,1)}), bf16[8,32,512]{2,1,0:T(8,128)(2,1)S(1)}, u32[]{:S(2)}, u32[]{:S(2)}) %all-to-all-start.1) | async-done | bytes 262176 | tf_op jit(solution)/shard_map/all_to_all | solution.py:352
  71.4 1.3 %collective-permute-start.3 = (bf16[256,512]{1,0:T(8,128)(2,1)S(1)}, bf16[256,512]{1,0:T(8,128)(2,1)S(1)}, u32[]{:S(2)}, u32[]{:S(2)}) collective-permute-start(bf16[256,512]{1,0:T(8,128)(2,1)S(1)} %bitcast.28), channel_id=1, source_target_pairs={{0,192},{64,0},{128,64},{192,128},{1,193},{65,1},{129,65},{193,129... | collective-permute-start | bytes 786440 | tf_op jit(solution)/shard_map/ppermute | solution.py:343
  73.8 1.4 %collective-permute-start.5 = (bf16[256,512]{1,0:T(8,128)(2,1)S(1)}, bf16[256,512]{1,0:T(8,128)(2,1)S(1)}, u32[]{:S(2)}, u32[]{:S(2)}) collective-permute-start(bf16[256,512]{1,0:T(8,128)(2,1)S(1)} %bitcast.30), channel_id=1, source_target_pairs={{0,64},{64,128},{128,192},{192,0},{1,65},{65,129},{129,193},{193,1... | collective-permute-start | bytes 786440 | tf_op jit(solution)/shard_map/ppermute | solution.py:343
  75.3 6.2 %count_matrix.3 = bf16[2048,2048]{1,0:T(8,128)(2,1)S(1)} custom-call(s32[8,2048]{1,0:T(8,128)S(1)} %get-tuple-element.24.nbrs_ref, s32[1,2048]{1,0:T(1,128)S(1)} %get-tuple-element.25.count_ref), custom_call_target="tpu_custom_call" | custom-call | flops 6710886400 | bytes 8388608 | tf_op jit(solution)/shard_map/count_matrix/pallas_call | solution.py:166
  81.5 1.6 %count_matrix.5.mat_ref = bf16[512,2048]{1,0:T(8,128)(2,1)S(1)} custom-call(s32[8,2048]{1,0:T(8,128)S(1)} %get-tuple-element.24.nbrs_ref, s32[1,2048]{1,0:T(1,128)S(1)} %get-tuple-element.25.count_ref), custom_call_target="tpu_custom_call" | custom-call | flops 1677721600 | bytes 2097152 | tf_op jit(solution)/shard_map/count_matrix/pallas_call | solution.py:166
  84.5 2.3 %fusion.15.total_ref = f32[256,2048]{1,0:T(8,128)S(1)} fusion(bf16[256,2048]{1,0:T(8,128)(2,1)S(1)} %fusion.3.hidden_ref, bf16[2048,2048]{1,0:T(8,128)(2,1)S(1)} %count_matrix.3), kind=kOutput, calls=%fused_computation.31 | convolution fusion | flops 2147483648 | bytes 11534336 | tf_op jit(solution)/shard_map/dot_general | solution.py:19
  86.8 4.7 %collective-permute-done.9.received_ref = bf16[256,512]{1,0:T(8,128)(2,1)S(1)} collective-permute-done((bf16[256,512]{1,0:T(8,128)(2,1)S(1)}, bf16[256,512]{1,0:T(8,128)(2,1)S(1)}, u32[]{:S(2)}, u32[]{:S(2)}) %collective-permute-start.9) | collective-permute-done | bytes 262176 | tf_op jit(solution)/shard_map/ppermute | solution.py:343
  91.5 8.1 %mlp.1 = (bf16[256,512]{1,0:T(8,128)(2,1)S(1)}, f32[256,2048]{1,0:T(8,128)S(1)}, bf16[256,2048]{1,0:T(8,128)(2,1)S(1)}, bf16[256,512]{1,0:T(8,128)(2,1)S(1)}) custom-call(f32[256,2048]{1,0:T(8,128)S(1)} %fusion.15.total_ref, bf16[256,512]{1,0:T(8,128)(2,1)S(1)} %collective-permute-done.9.received_ref, bf16[512,2048]{1,0:T(8,128)(2,1)S(1)} %count_matrix.5.mat_ref, ...), custom_call_target="tpu_custom_call" | custom-call | flops 3221225472 | bytes 20971520 | tf_op jit(solution)/shard_map/mlp/pallas_call | solution.py:278
  99.7 2.4 %fusion.16 = f32[256,2048]{1,0:T(8,128)S(1)} fusion(bf16[256,2048]{1,0:T(8,128)(2,1)S(1)} %get-tuple-element.27, bf16[2048,2048]{1,0:T(8,128)(2,1)S(1)} %count_matrix.3), kind=kOutput, calls=%fused_computation.32 | convolution fusion | flops 2147483648 | bytes 11534336 | tf_op jit(solution)/shard_map/dot_general | solution.py:23
  103.6 2.1 %last.1 = (f32[160,256]{1,0:T(8,128)S(1)}, f32[160,256]{1,0:T(8,128)}) custom-call(s32[1]{0:T(128)} %bitcast.core_ref, f32[256,2048]{1,0:T(8,128)S(1)} %add.63.part_ref, bf16[256,512]{1,0:T(8,128)(2,1)S(1)} %collective-permute-done.17.returned_ref, bf16[2048,512]{1,0:T(8,128)(2,1)S(1)} %count_matrix.4.pick_ref, bf16[256,512]{1,0:T(8,128)(2,1)S(1)} %bitcast.32, ...), custom_call_target="tpu_custom_call" | custom-call | flops 4294967296 | bytes 8388608 | tf_op jit(solution)/shard_map/last/pallas_call | solution.py:334
  106.8 1.2 %collective-permute-done.18 = f32[160,256]{1,0:T(8,128)S(1)} collective-permute-done((f32[160,256]{1,0:T(8,128)}, f32[160,256]{1,0:T(8,128)S(1)}, u32[]{:S(2)}, u32[]{:S(2)}) %collective-permute-start.18) | collective-permute-done | bytes 163872 | tf_op jit(solution)/shard_map/ppermute | solution.py:347
  109.0 1.6 %collective-permute-start.19 = (bf16[160,256]{1,0:T(8,128)(2,1)S(1)}, bf16[160,256]{1,0:T(8,128)(2,1)S(1)}, u32[]{:S(2)}, u32[]{:S(2)}) collective-permute-start(bf16[160,256]{1,0:T(8,128)(2,1)S(1)} %add_convert_fusion.1), channel_id=1, source_target_pairs={{0,2},{2,0},{4,6},{6,4},{1,3},{3,1},{5,7},{7,5},{8,10},{10,8},{12,... | collective-permute-start | bytes 245768 | tf_op jit(solution)/shard_map/ppermute | solution.py:347
  110.6 2.9 %collective-permute-start.20 = (bf16[160,256]{1,0:T(8,128)(2,1)S(1)}, bf16[160,256]{1,0:T(8,128)(2,1)S(1)}, u32[]{:S(2)}, u32[]{:S(2)}) collective-permute-start(bf16[160,256]{1,0:T(8,128)(2,1)S(1)} %add_convert_fusion.1), channel_id=1, source_target_pairs={{0,4},{2,6},{4,0},{6,2},{1,5},{3,7},{5,1},{7,3},{8,12},{10,14},{12... | collective-permute-start | bytes 245768 | tf_op jit(solution)/shard_map/ppermute | solution.py:347
  113.8 1.8 %fusion.4 = bf16[64,256]{0,1:T(8,128)(2,1)S(1)} fusion(bf16[1024,256]{1,0:T(8,128)(2,1)} %w_out_ref.1, bf16[256,1024]{1,0:T(8,128)(2,1)} %w_in_ref.1, bf16[256,512]{1,0:T(8,128)(2,1)} %copy-done.8, s32[]{:T(128)S(6)} %select_n.64, bf16[256,2048]{1,0:T(8,128)(2,1)S(1)} %fusion.3.hidden_ref, s32[]{:T(128)S(6)} %select_n.63), kind=kOutput, calls=%fused_computation.8 | convolution fusion | flops 67485696 | bytes 1179656 | tf_op jit(solution)/shard_map/dot_general | solution.py:19
  115.6 2.4 %collective-permute-done.20 = bf16[160,256]{1,0:T(8,128)(2,1)S(1)} collective-permute-done((bf16[160,256]{1,0:T(8,128)(2,1)S(1)}, bf16[160,256]{1,0:T(8,128)(2,1)S(1)}, u32[]{:S(2)}, u32[]{:S(2)}) %collective-permute-start.20) | collective-permute-done | bytes 81952 | tf_op jit(solution)/shard_map/ppermute | solution.py:347
  118.0 1.7 %collective-permute-done.21 = bf16[160,256]{1,0:T(8,128)(2,1)S(1)} collective-permute-done((bf16[160,256]{1,0:T(8,128)(2,1)S(1)}, bf16[160,256]{1,0:T(8,128)(2,1)S(1)}, u32[]{:S(2)}, u32[]{:S(2)}) %collective-permute-start.21) | collective-permute-done | bytes 81952 | tf_op jit(solution)/shard_map/ppermute | solution.py:347
  (88 shorter events, 17.2 us)
Async XLA Ops:
  9.0 26.8 %collective-permute-start.1 = (bf16[256,512]{1,0:T(8,128)(2,1)}, bf16[256,512]{1,0:T(8,128)(2,1)S(1)}, u32[]{:S(2)}, u32[]{:S(2)}) collective-permute-start(bf16[256,512]{1,0:T(8,128)(2,1)} %get-tuple-element.21), channel_id=1, source_target_pairs={{0,64},{64,128},{128,192},{192,0},{1,65},{65,129},{129,193},{193,1... | collective-permute-start | bytes 786440 | tf_op jit(solution)/shard_map/ppermute | solution.py:343
  10.7 8.5 %copy-start.13 = (bf16[64,256]{1,0:T(8,128)(2,1)S(1)}, bf16[64,256]{1,0:T(8,128)(2,1)}, u32[]{:S(2)}) copy-start(bf16[64,256]{1,0:T(8,128)(2,1)} %param.21) | copy-start | bytes 98308
  10.7 25.1 %collective-permute-start.2 = (bf16[256,512]{1,0:T(8,128)(2,1)}, bf16[256,512]{1,0:T(8,128)(2,1)S(1)}, u32[]{:S(2)}, u32[]{:S(2)}) collective-permute-start(bf16[256,512]{1,0:T(8,128)(2,1)} %get-tuple-element.22), channel_id=1, source_target_pairs={{0,192},{64,0},{128,64},{192,128},{1,193},{65,1},{129,65},{193,129... | collective-permute-start | bytes 786440 | tf_op jit(solution)/shard_map/ppermute | solution.py:343
  17.0 9.7 %copy-start.1 = (bf16[256,1024]{1,0:T(8,128)(2,1)S(1)}, bf16[256,1024]{1,0:T(8,128)(2,1)}, u32[]{:S(2)}) copy-start(bf16[256,1024]{1,0:T(8,128)(2,1)} %w_in_ref.1) | copy-start | bytes 1572868
  17.0 10.8 %copy-start.5 = (s32[64,8]{0,1:T(8,128)S(1)}, s32[64,8]{0,1:T(8,128)}, u32[]{:S(2)}) copy-start(s32[64,8]{0,1:T(8,128)} %param.17) | copy-start | bytes 6148
  17.0 10.7 %copy-start.6 = (s32[64]{0:T(128)S(1)}, s32[64]{0:T(128)}, u32[]{:S(2)}) copy-start(s32[64]{0:T(128)} %param.18) | copy-start | bytes 772
  17.0 10.8 %copy-start.15 = (f32[256]{0:T(256)S(1)}, f32[256]{0:T(256)}, u32[]{:S(2)}) copy-start(f32[256]{0:T(256)} %param.15) | copy-start | bytes 3076
  17.0 18.8 %collective-permute-start = (bf16[256,512]{1,0:T(8,128)(2,1)}, bf16[256,512]{1,0:T(8,128)(2,1)S(1)}, u32[]{:S(2)}, u32[]{:S(2)}) collective-permute-start(bf16[256,512]{1,0:T(8,128)(2,1)} %get-tuple-element.20), channel_id=1, source_target_pairs={{0,128},{64,192},{128,0},{192,64},{1,129},{65,193},{129,1},{193,65... | collective-permute-start | bytes 786440 | tf_op jit(solution)/shard_map/ppermute | solution.py:343
  19.2 8.7 %collective-permute-start.10 = (bf16[64,256]{1,0:T(8,128)(2,1)S(1)}, bf16[64,256]{1,0:T(8,128)(2,1)S(1)}, u32[]{:S(2)}, u32[]{:S(2)}) collective-permute-start(bf16[64,256]{1,0:T(8,128)(2,1)S(1)} %copy-done.13), channel_id=1, source_target_pairs={{0,8},{8,0},{16,24},{24,16},{32,40},{40,32},{48,56},{56,48},{1,9},... | collective-permute-start | bytes 98312 | tf_op jit(solution)/shard_map/ppermute | solution.py:347
  27.9 16.1 %collective-permute-start.11 = (bf16[128,256]{1,0:T(8,128)(2,1)S(1)}, bf16[128,256]{1,0:T(8,128)(2,1)S(1)}, u32[]{:S(2)}, u32[]{:S(2)}) collective-permute-start(bf16[128,256]{1,0:T(8,128)(2,1)S(1)} %maximum_select_fusion.1), channel_id=1, source_target_pairs={{0,16},{8,24},{16,0},{24,8},{32,48},{40,56},{48,32},{56,40},{1,17}... | collective-permute-start | bytes 196616 | tf_op jit(solution)/shard_map/ppermute | solution.py:347
  31.3 12.7 %collective-permute-start.12 = (bf16[128,256]{1,0:T(8,128)(2,1)S(1)}, bf16[128,256]{1,0:T(8,128)(2,1)S(1)}, u32[]{:S(2)}, u32[]{:S(2)}) collective-permute-start(bf16[128,256]{1,0:T(8,128)(2,1)S(1)} %maximum_select_fusion.1), channel_id=1, source_target_pairs={{0,32},{8,40},{16,48},{24,56},{32,0},{40,8},{48,16},{56,24},{1,33}... | collective-permute-start | bytes 196616 | tf_op jit(solution)/shard_map/ppermute | solution.py:347
  35.8 8.2 %collective-permute-start.13 = (bf16[128,256]{1,0:T(8,128)(2,1)S(1)}, bf16[128,256]{1,0:T(8,128)(2,1)S(1)}, u32[]{:S(2)}, u32[]{:S(2)}) collective-permute-start(bf16[128,256]{1,0:T(8,128)(2,1)S(1)} %maximum_select_fusion.1), channel_id=1, source_target_pairs={{0,48},{8,56},{16,32},{24,40},{32,16},{40,24},{48,0},{56,8},{1,49}... | collective-permute-start | bytes 196616 | tf_op jit(solution)/shard_map/ppermute | solution.py:347
  36.9 24.1 %copy-start.14 = (s32[512]{0:T(512)S(1)}, s32[512]{0:T(512)}, u32[]{:S(2)}) copy-start(s32[512]{0:T(512)} %param.16) | copy-start | bytes 6148
  37.7 19.0 %all-to-all-start = ((bf16[8,48,512]{2,1,0:T(8,128)(2,1)}), bf16[8,48,512]{2,1,0:T(8,128)(2,1)S(1)}, u32[]{:S(2)}, u32[]{:S(2)}) async-start(bf16[8,48,512]{2,1,0:T(8,128)(2,1)} %pad_maximum_fusion.1), calls=%async_computation | async-start | bytes 786432 | tf_op jit(solution)/shard_map/all_to_all | solution.py:400
  44.2 19.8 %collective-permute-start.14 = (bf16[512,256]{1,0:T(8,128)(2,1)S(1)}, bf16[512,256]{1,0:T(8,128)(2,1)S(1)}, u32[]{:S(2)}, u32[]{:S(2)}) collective-permute-start(bf16[512,256]{1,0:T(8,128)(2,1)S(1)} %bitcast.39), channel_id=1, source_target_pairs={{0,192},{64,0},{128,64},{192,128},{1,193},{65,1},{129,65},{193,129... | collective-permute-start | bytes 786440 | tf_op jit(solution)/shard_map/ppermute | solution.py:343
  45.6 19.8 %collective-permute-start.15 = (bf16[512,256]{1,0:T(8,128)(2,1)S(1)}, bf16[512,256]{1,0:T(8,128)(2,1)}, u32[]{:S(2)}, u32[]{:S(2)}) collective-permute-start(bf16[512,256]{1,0:T(8,128)(2,1)S(1)} %bitcast.40), channel_id=1, source_target_pairs={{0,128},{64,192},{128,0},{192,64},{1,129},{65,193},{129,1},{193,65... | collective-permute-start | bytes 786440 | tf_op jit(solution)/shard_map/ppermute | solution.py:343
  46.6 18.9 %collective-permute-start.16 = (bf16[512,256]{1,0:T(8,128)(2,1)S(1)}, bf16[512,256]{1,0:T(8,128)(2,1)}, u32[]{:S(2)}, u32[]{:S(2)}) collective-permute-start(bf16[512,256]{1,0:T(8,128)(2,1)S(1)} %bitcast.41), channel_id=1, source_target_pairs={{0,64},{64,128},{128,192},{192,0},{1,65},{65,129},{129,193},{193,1... | collective-permute-start | bytes 786440 | tf_op jit(solution)/shard_map/ppermute | solution.py:343
  57.6 13.8 %all-to-all-start.1 = ((bf16[8,32,512]{2,1,0:T(8,128)(2,1)}), bf16[8,32,512]{2,1,0:T(8,128)(2,1)S(1)}, u32[]{:S(2)}, u32[]{:S(2)}) async-start(bf16[8,32,512]{2,1,0:T(8,128)(2,1)} %broadcast_in_dim.28), calls=%async_computation.1 | async-start | bytes 524288 | tf_op jit(solution)/shard_map/all_to_all | solution.py:352
  61.5 6.0 %collective-permute-start.6 = (bf16[8,16,256]{2,1,0:T(8,128)(2,1)S(1)}, bf16[8,16,256]{2,1,0:T(8,128)(2,1)S(1)}, u32[]{:S(2)}, u32[]{:S(2)}) collective-permute-start(bf16[8,16,256]{2,1,0:T(8,128)(2,1)S(1)} %slice.9.refs_0_), channel_id=1, source_target_pairs={{0,192},{64,0},{128,64},{192,128},{1,193},{65,1},{129,65},{193,129... | collective-permute-start | bytes 196616 | tf_op jit(solution)/shard_map/ppermute | solution.py:343
  62.9 5.8 %collective-permute-start.7 = (bf16[8,16,256]{2,1,0:T(8,128)(2,1)S(1)}, bf16[8,16,256]{2,1,0:T(8,128)(2,1)S(1)}, u32[]{:S(2)}, u32[]{:S(2)}) collective-permute-start(bf16[8,16,256]{2,1,0:T(8,128)(2,1)S(1)} %slice.9.refs_0_), channel_id=1, source_target_pairs={{0,128},{64,192},{128,0},{192,64},{1,129},{65,193},{129,1},{193,65... | collective-permute-start | bytes 196616 | tf_op jit(solution)/shard_map/ppermute | solution.py:343
  64.0 4.7 %collective-permute-start.8 = (bf16[8,16,256]{2,1,0:T(8,128)(2,1)S(1)}, bf16[8,16,256]{2,1,0:T(8,128)(2,1)S(1)}, u32[]{:S(2)}, u32[]{:S(2)}) collective-permute-start(bf16[8,16,256]{2,1,0:T(8,128)(2,1)S(1)} %slice.9.refs_0_), channel_id=1, source_target_pairs={{0,64},{64,128},{128,192},{192,0},{1,65},{65,129},{129,193},{193,1... | collective-permute-start | bytes 196616 | tf_op jit(solution)/shard_map/ppermute | solution.py:343
  71.4 11.7 %collective-permute-start.3 = (bf16[256,512]{1,0:T(8,128)(2,1)S(1)}, bf16[256,512]{1,0:T(8,128)(2,1)S(1)}, u32[]{:S(2)}, u32[]{:S(2)}) collective-permute-start(bf16[256,512]{1,0:T(8,128)(2,1)S(1)} %bitcast.28), channel_id=1, source_target_pairs={{0,192},{64,0},{128,64},{192,128},{1,193},{65,1},{129,65},{193,129... | collective-permute-start | bytes 786440 | tf_op jit(solution)/shard_map/ppermute | solution.py:343
  72.7 10.3 %collective-permute-start.4 = (bf16[256,512]{1,0:T(8,128)(2,1)S(1)}, bf16[256,512]{1,0:T(8,128)(2,1)S(1)}, u32[]{:S(2)}, u32[]{:S(2)}) collective-permute-start(bf16[256,512]{1,0:T(8,128)(2,1)S(1)} %bitcast.29), channel_id=1, source_target_pairs={{0,128},{64,192},{128,0},{192,64},{1,129},{65,193},{129,1},{193,65... | collective-permute-start | bytes 786440 | tf_op jit(solution)/shard_map/ppermute | solution.py:343
  73.8 9.3 %collective-permute-start.5 = (bf16[256,512]{1,0:T(8,128)(2,1)S(1)}, bf16[256,512]{1,0:T(8,128)(2,1)S(1)}, u32[]{:S(2)}, u32[]{:S(2)}) collective-permute-start(bf16[256,512]{1,0:T(8,128)(2,1)S(1)} %bitcast.30), channel_id=1, source_target_pairs={{0,64},{64,128},{128,192},{192,0},{1,65},{65,129},{129,193},{193,1... | collective-permute-start | bytes 786440 | tf_op jit(solution)/shard_map/ppermute | solution.py:343
  84.4 7.1 %copy-start = (bf16[2048,256]{1,0:T(8,128)(2,1)S(1)}, bf16[2048,256]{1,0:T(8,128)(2,1)}, u32[]{:S(2)}) copy-start(bf16[2048,256]{1,0:T(8,128)(2,1)} %pad_maximum_fusion.cot_ref) | copy-start | bytes 3145732
  84.5 7.0 %collective-permute-start.9 = (bf16[256,512]{1,0:T(8,128)(2,1)S(1)}, bf16[256,512]{1,0:T(8,128)(2,1)S(1)}, u32[]{:S(2)}, u32[]{:S(2)}) collective-permute-start(bf16[256,512]{1,0:T(8,128)(2,1)S(1)} %convolution_convert_fusion), channel_id=1, source_target_pairs={{0,1},{1,2},{2,3},{3,4},{4,5},{5,6},{6,7},{7,0},{8,9},{9,10},{10,1... | collective-permute-start | bytes 786440 | tf_op jit(solution)/shard_map/ppermute | solution.py:343
  99.6 3.9 %collective-permute-start.17 = (bf16[256,512]{1,0:T(8,128)(2,1)S(1)}, bf16[256,512]{1,0:T(8,128)(2,1)S(1)}, u32[]{:S(2)}, u32[]{:S(2)}) collective-permute-start(bf16[256,512]{1,0:T(8,128)(2,1)S(1)} %get-tuple-element.28), channel_id=1, source_target_pairs={{0,7},{1,0},{2,1},{3,2},{4,3},{5,4},{6,5},{7,6},{8,15},{9,8},{10,9... | collective-permute-start | bytes 786440 | tf_op jit(solution)/shard_map/ppermute | solution.py:343
  106.3 1.8 %collective-permute-start.18 = (f32[160,256]{1,0:T(8,128)}, f32[160,256]{1,0:T(8,128)S(1)}, u32[]{:S(2)}, u32[]{:S(2)}) collective-permute-start(f32[160,256]{1,0:T(8,128)} %get-tuple-element.34), channel_id=1, source_target_pairs={{0,1},{1,0},{2,3},{3,2},{4,5},{5,4},{6,7},{7,6},{8,9},{9,8},{10,11... | collective-permute-start | bytes 491528 | tf_op jit(solution)/shard_map/ppermute | solution.py:347
  109.0 6.6 %collective-permute-start.19 = (bf16[160,256]{1,0:T(8,128)(2,1)S(1)}, bf16[160,256]{1,0:T(8,128)(2,1)S(1)}, u32[]{:S(2)}, u32[]{:S(2)}) collective-permute-start(bf16[160,256]{1,0:T(8,128)(2,1)S(1)} %add_convert_fusion.1), channel_id=1, source_target_pairs={{0,2},{2,0},{4,6},{6,4},{1,3},{3,1},{5,7},{7,5},{8,10},{10,8},{12,... | collective-permute-start | bytes 245768 | tf_op jit(solution)/shard_map/ppermute | solution.py:347
  110.6 7.5 %collective-permute-start.20 = (bf16[160,256]{1,0:T(8,128)(2,1)S(1)}, bf16[160,256]{1,0:T(8,128)(2,1)S(1)}, u32[]{:S(2)}, u32[]{:S(2)}) collective-permute-start(bf16[160,256]{1,0:T(8,128)(2,1)S(1)} %add_convert_fusion.1), channel_id=1, source_target_pairs={{0,4},{2,6},{4,0},{6,2},{1,5},{3,7},{5,1},{7,3},{8,12},{10,14},{12... | collective-permute-start | bytes 245768 | tf_op jit(solution)/shard_map/ppermute | solution.py:347
  113.5 6.2 %collective-permute-start.21 = (bf16[160,256]{1,0:T(8,128)(2,1)S(1)}, bf16[160,256]{1,0:T(8,128)(2,1)S(1)}, u32[]{:S(2)}, u32[]{:S(2)}) collective-permute-start(bf16[160,256]{1,0:T(8,128)(2,1)S(1)} %add_convert_fusion.1), channel_id=1, source_target_pairs={{0,6},{2,4},{4,2},{6,0},{1,7},{3,5},{5,3},{7,1},{8,14},{10,12},{12... | collective-permute-start | bytes 245768 | tf_op jit(solution)/shard_map/ppermute | solution.py:347
  119.8 1.5 %collective-permute-start.22 = (f32[160,256]{1,0:T(8,128)S(1)}, f32[160,256]{1,0:T(8,128)S(1)}, u32[]{:S(2)}, u32[]{:S(2)}) collective-permute-start(f32[160,256]{1,0:T(8,128)S(1)} %add_add_fusion), channel_id=1, source_target_pairs={{0,1},{1,0},{2,3},{3,2},{4,5},{5,4},{6,7},{7,6},{8,9},{9,8},{10,11... | collective-permute-start | bytes 491528 | tf_op jit(solution)/shard_map/ppermute | solution.py:347
  (9 other events, 30.2 us)
